TPU v7x, 512 devices: a whole 4x4x16 slice. The times are simulated.
512 devices in a mesh: ctx: 64 (over z, x_hi, core), head: 8 (over y, x_lo).
Axes of the slice: x: 4 (x_hi: 2, x_lo: 2; x = x_hi * 2 + x_lo), y: 4, z: 16, core: 2. Of those that a mesh axis runs over, the one named last changes fastest.
Arguments:
- queries: bfloat16 [16384, 4096], P('ctx', 'head'), may hold values from -6 to 6
- keys: bfloat16 [16384, 1024], P('ctx', 'head'), may hold values from -6 to 6
- values: bfloat16 [16384, 1024], P('ctx', 'head'), may hold values from -36 to 36
- cotangent: bfloat16 [16384, 4096], P('ctx', 'head'), may hold values from -6 to 6
- gain: float32 [4096], P('head'), may hold values from 0.1 to 1.9
- key_blocks: int32 [128, 20], replicated, may hold values from -1 to 126, as said below
- span_order: int32 [128], replicated, may hold values from 0 to 127, as said below
Outputs:
- output: bfloat16 [16384, 4096], P('ctx', 'head')
- query_grad: bfloat16 [16384, 4096], P('ctx', 'head')
- key_grad: bfloat16 [16384, 1024], P('ctx', 'head')
- value_grad: bfloat16 [16384, 1024], P('ctx', 'head')
Inputs may be any that keep to these rules, and one draw needn't show every extreme that they name: `span_order`: a permutation of the storage blocks' sequence blocks. `key_blocks`: row b names distinct sequence blocks, each less than b, and -1 in empty slots, which come last in a row. Over the rows of the sequence blocks held by the 2 storage blocks of one device, the named blocks never include two different blocks that lie on one same device.
All inputs are finite; a program needn't handle non-finite values.
Results may differ from a plain program's by a relative error of at most 0.0058.
Values may be sent and summed in bfloat16 or wider, within the bound.
No kernel may reach another device: no remote copies, remote signals or barrier semaphores. Data moves between devices by JAX's collectives and lax.ppermute only.
A program may use at most 64 MiB of HBM per device.

v0:
```python
import math

import jax
import jax.numpy as jnp
from jax import lax
from jax.experimental import pallas as pl
from jax.experimental.pallas import tpu as pltpu
from jax.sharding import Mesh, PartitionSpec as P


DH = 128
BLOCK = 128
CTX = ("z", "xh", "core")
HEAD = ("y", "xl")
RING = ("z", "core")
NZ = 16
HALF = NZ // 2
SWAP = [(0, 1), (1, 0)]
NBLK = 128
PART = 4 * BLOCK
SWAP_AFTER = (2, 4, 6, 7)
GATHERED = [1] * 16 + [4, 4, 4, 2, 1, 1]
SENT = [16, 6, 4, 4, 1, 1]
F32 = jnp.float32
BF16 = jnp.bfloat16


def ring_pairs():
    return [
        (z * 2 + c, ((z + (1 if c == 0 else -1)) % NZ) * 2 + c) for z in range(NZ) for c in range(2)
    ]


def ring(x):
    return lax.ppermute(x, RING, ring_pairs())


def swap(x):
    return lax.ppermute(x, "core", SWAP)


def gather_blocks(kv):
    pair = jnp.concatenate([kv, lax.ppermute(kv, "xh", SWAP)], axis=0)
    own, other = pair, swap(pair)
    chunk, mine, theirs = [own, other], [], []
    waiting = []
    for s in range(1, HALF):
        own, other = ring(own), ring(other)
        mine += [own, other]
        waiting += [other, own]
        if s in SWAP_AFTER:
            theirs.append(swap(jnp.concatenate(waiting, axis=0)))
            waiting = []
    return chunk + mine + theirs + [ring(own), ring(other)]


def total(*terms):
    out = terms[0].astype(F32)
    for t in terms[1:]:
        out = out + t.astype(F32)
    return out


def part_of(array, i):
    return array[i * PART : (i + 1) * PART]


def scatter_blocks(mine, near, middle, distant, *far):
    own, other = far
    near, middle, distant = swap(near), swap(middle), swap(distant)
    for s in range(HALF - 1, 0, -1):
        theirs, base = (distant, 6) if s > 5 else (middle, 4) if s > 3 else (near, 1)
        i = 2 * (s - base)
        other = ring(other)
        other = total(other, part_of(mine, 2 * s + 1), part_of(theirs, i)).astype(BF16)
        other, later_mine, later_theirs = lax.optimization_barrier((other, mine, theirs))
        own = ring(own)
        own = total(own, part_of(later_mine, 2 * s), part_of(later_theirs, i + 1)).astype(BF16)
    other = total(ring(other), part_of(mine, 1)).astype(BF16)
    own = ring(own)
    keep = total(own, part_of(mine, 0), swap(other))
    rows = PART // 2
    mate = lax.ppermute(keep[rows:].astype(BF16), "xh", SWAP)
    return keep[:rows] + mate.astype(F32)


def head_copies(x):
    return lax.all_to_all(x, HEAD, 0, 0, tiled=True)


def positions(key_blocks, span_order, per_device):
    z, xh, core = (lax.axis_index(n) for n in CTX)
    me = (z * 2 + xh) * 2 + core
    seq = lax.dynamic_slice(span_order, (me * per_device,), (per_device,))
    pick = (seq[:, None] == jnp.arange(NBLK)[None, :]).astype(jnp.int32)
    far = jnp.sum(pick[:, :, None] * key_blocks[None], axis=1)
    where = jnp.arange(NBLK, dtype=jnp.int32)
    store = jnp.sum(
        jnp.where(far[:, :, None] == span_order[None, None, :], where[None, None, :], 0), axis=2
    )
    own = me * per_device + jnp.arange(per_device, dtype=jnp.int32)
    store = jnp.concatenate([own[:, None], store], axis=1)
    live = jnp.concatenate([jnp.ones((per_device, 1), bool), far >= 0], axis=1)
    owner, half = store // per_device, store % per_device
    oz, oxh, ocore = owner // 4, (owner // 2) % 2, owner % 2
    dz = (oz - z + HALF) % NZ - HALF
    inner = (oxh ^ xh) * 2 + half
    dist = jnp.abs(dz)

    across = ocore ^ core

    def locate(first_group):
        chunk = jnp.where(first_group, 0, 14) + 2 * dist
        chunk = jnp.where(dist == 0, 0, jnp.where(dist == HALF, 30, chunk))
        return jnp.where(live, (chunk + across) * 4 + inner, NBLK).reshape(-1)

    def holder(spot):
        match = spot[None, :] == jnp.arange(NBLK, dtype=jnp.int32)[:, None]
        return jnp.max(jnp.where(match, slot[None, :], -1), axis=1)

    source = locate((dz < 0) == (core == 0))
    count = source.shape[0]
    order = jnp.arange(count, dtype=jnp.int32)
    same = source[:, None] == source[None, :]
    first = jnp.min(jnp.where(same, order[None, :], count), axis=1)
    slot = jnp.where(source == NBLK, count, first).astype(jnp.int32)
    back = locate((dz > 0) == (core == 0))
    return slot.reshape(per_device, -1), holder(source), holder(back)


def rows_of(spot):
    return pl.ds(pl.multiple_of(spot * BLOCK, BLOCK), BLOCK)


def contract_first(a, b):
    return lax.dot_general(a, b, (((0,), (0,)), ((), ())), preferred_element_type=F32)


def dot(a, b):
    return jnp.dot(a, b, preferred_element_type=F32)


def heads_of(ref, q, n):
    return [ref[pl.ds(q * BLOCK, BLOCK), h * DH : (h + 1) * DH] for h in range(n)]


def each_block(counts, visit):
    base = 0
    for k, n in enumerate(counts):

        def one(i, carry, k=k, base=base):
            visit(k, i, base + i)
            return carry

        lax.fori_loop(0, 4 * n, one, 0)
        base += 4 * n


def steps_at(i):
    if isinstance(i, int) and i == 0:
        return 0, BLOCK
    return pl.multiple_of(BLOCK + 2 * BLOCK * (i - 1), BLOCK), 2 * BLOCK


def causal_mask(width):
    key = lax.broadcasted_iota(jnp.int32, (BLOCK, width), 0)
    row = lax.broadcasted_iota(jnp.int32, (BLOCK, width), 1) % BLOCK
    return key <= row


def forward_kernel(pairs, scale, shift, slots, holder, queries, cotangent, gain, *rest):
    n = len(GATHERED)
    sources, (attended, weights, held, sums, sems) = rest[:n], rest[n:]
    per_device = slots.shape[0]
    spare = per_device * slots.shape[1]
    group = queries.shape[1] // DH
    width = group * BLOCK

    def fetch(k, i, at):
        @pl.when(holder[at] >= 0)
        def _():
            pltpu.make_async_copy(
                sources[k].at[rows_of(i), :], held.at[rows_of(holder[at]), :], sems.at[holder[at]]
            ).start()

    def await_slot(q, j):
        mine = slots[q, j]

        @pl.when(mine == q * slots.shape[1] + j)
        def _():
            pltpu.make_async_copy(
                sources[0].at[:BLOCK, :], held.at[rows_of(mine), :], sems.at[mine]
            ).wait()

        return held[rows_of(mine), :]

    each_block(GATHERED, fetch)
    held[spare * BLOCK :, :] = jnp.zeros((BLOCK, 2 * DH), BF16)
    query_t = [
        jnp.concatenate([x.T for x in heads_of(queries, q, group)], axis=1)
        for q in range(per_device)
    ]

    def weigh(keys, query):
        score = dot(keys, query)
        return 1.0 / (1.0 + jnp.exp(shift - score * scale))

    for q in range(per_device):
        own = await_slot(q, 0)
        weight = jnp.where(causal_mask(width), weigh(own[:, :DH], query_t[q]), 0.0)
        weights[q, :BLOCK, :] = weight
        attended[q] = contract_first(own[:, DH:], weight.astype(BF16))

        def step(i, carry):
            two = jnp.concatenate([await_slot(q, 1 + 2 * i), await_slot(q, 2 + 2 * i)], axis=0)
            weight = weigh(two[:, :DH], query_t[q])
            weights[q, pl.ds(*steps_at(i + 1)), :] = weight
            attended[q] += contract_first(two[:, DH:], weight.astype(BF16))
            return carry

        lax.fori_loop(0, pairs, step, 0, unroll=True)
        att = attended[q]
        grad_in = jnp.concatenate(
            [
                (x.astype(F32) * gain[:, h * DH : (h + 1) * DH]).T
                for h, x in enumerate(heads_of(cotangent, q, group))
            ],
            axis=1,
        )
        for i, value in enumerate((att * att, grad_in * att)):
            col = jnp.sum(value, axis=0, keepdims=True)
            row = col[:, :BLOCK]
            for h in range(1, group):
                row = row + col[:, h * BLOCK : (h + 1) * BLOCK]
            sums[:, 2 * q + i : 2 * q + i + 1, :] = jnp.broadcast_to(
                row[None], (sums.shape[0], 1, BLOCK)
            )


def backward_kernel(
    pairs, scale, columns, slots, holder, sums, queries, cotangent, gain, attended, weights, held, *rest
):
    m = len(SENT)
    output, query_grad = rest[:2]
    parts = rest[2 : m + 2]
    acc = rest[m + 2]
    per_device, count = slots.shape
    group = queries.shape[1] // DH
    for part in parts:
        part[...] = jnp.zeros(part.shape, BF16)
    grads_t, grads, stacked = [], [], []
    for q in range(per_device):
        inverse = lax.rsqrt(jnp.sum(sums[:, 2 * q, :], axis=0, keepdims=True) / columns + 1e-6)
        inner = jnp.sum(sums[:, 2 * q + 1, :], axis=0, keepdims=True) / columns
        back = inverse * inverse * inner
        grad_t, grad = [], []
        for h, x in enumerate(heads_of(cotangent, q, group)):
            gain_h = gain[:, h * DH : (h + 1) * DH]
            att = attended[q, :, h * BLOCK : (h + 1) * BLOCK]
            grad_in = (x.astype(F32) * gain_h).T
            low = inverse * (grad_in - att * back)
            grad_t.append(low.astype(BF16))
            grad.append(low.T.astype(BF16))
            output[pl.ds(q * BLOCK, BLOCK), h * DH : (h + 1) * DH] = (
                (att * inverse).T * gain_h
            ).astype(BF16)
        grads_t.append(jnp.concatenate(grad_t, axis=1))
        grads.append(jnp.concatenate(grad, axis=0))
        stacked.append(jnp.concatenate(heads_of(queries, q, group), axis=0))

    def pair_grads(q, both, weight):
        low = weight.astype(BF16)
        grad_weight = dot(both[:, DH:], grads_t[q])
        grad_score = (grad_weight * (weight * (1.0 - weight))).astype(BF16)
        part = jnp.concatenate([dot(grad_score, stacked[q]) * scale, dot(low, grads[q])], axis=1)
        return contract_first(both[:, :DH], grad_score), part

    def keep_part(q, j, part):
        slot = slots[q, j]
        if q > 0:
            again = slot < q * count
            part = part + jnp.where(again, acc[rows_of(slot), :], 0.0)
        acc[rows_of(slot), :] = part

    for q in range(per_device):
        own = held[rows_of(slots[q, 0]), :]
        query_part, part = pair_grads(q, own, weights[q, :BLOCK, :])
        keep_part(q, 0, part)

        def step(i, query_part):
            two = jnp.concatenate(
                [held[rows_of(slots[q, 1 + 2 * i]), :], held[rows_of(slots[q, 2 + 2 * i]), :]], axis=0
            )
            more, part = pair_grads(q, two, weights[q, pl.ds(*steps_at(i + 1)), :])
            keep_part(q, 1 + 2 * i, part[:BLOCK])
            keep_part(q, 2 + 2 * i, part[BLOCK:])
            return query_part + more

        query_part = lax.fori_loop(0, pairs, step, query_part, unroll=True)
        for h in range(group):
            query_grad[pl.ds(q * BLOCK, BLOCK), h * DH : (h + 1) * DH] = (
                query_part[:, h * BLOCK : (h + 1) * BLOCK].T * scale
            ).astype(BF16)

    def hand_over(k, i, at):
        @pl.when(holder[at] >= 0)
        def _():
            parts[k][rows_of(i), :] = acc[rows_of(holder[at]), :].astype(BF16)

    each_block(SENT, hand_over)


def specs():
    return tuple(pl.BlockSpec(memory_space=m) for m in (pltpu.SMEM, pltpu.VMEM, pltpu.HBM))


def sizes(queries, pos):
    per_device, slots = pos.shape
    wide = (queries.shape[1] // DH) * BLOCK
    flops = 2 * slots * per_device * wide * BLOCK * DH
    return per_device, slots, (slots - 1) // 2, wide, flops


def forward(heads, slots, holder, queries, cotangent, gain, gathered):
    per_device, count, pairs, wide, flops = sizes(queries, slots)
    smem, vmem, hbm = specs()
    gathered = [pltpu.with_memory_space_constraint(g, pltpu.HBM) for g in gathered]
    return pl.pallas_call(
        lambda *refs: forward_kernel(pairs, 1.0 / math.sqrt(DH), math.log(BLOCK * count), *refs),
        out_shape=(
            jax.ShapeDtypeStruct((per_device, DH, wide), F32),
            jax.ShapeDtypeStruct((per_device, count * BLOCK, wide), F32),
            jax.ShapeDtypeStruct(((per_device * count + 1) * BLOCK, 2 * DH), BF16),
            jax.ShapeDtypeStruct((heads, 2 * per_device, BLOCK), F32),
        ),
        in_specs=[smem, smem, vmem, vmem, vmem] + [hbm] * len(GATHERED),
        out_specs=(vmem,) * 4,
        scratch_shapes=[pltpu.SemaphoreType.DMA((per_device * count,))],
        compiler_params=pltpu.CompilerParams(vmem_limit_bytes=8 << 20),
        cost_estimate=pl.CostEstimate(flops=2 * flops, bytes_accessed=16 << 20, transcendentals=0),
        name="forward",
    )(slots, holder, queries, cotangent, gain, *gathered)


def backward(heads, slots, holder, sums, queries, cotangent, gain, attended, weights, held):
    per_device, count, pairs, _, flops = sizes(queries, slots)
    smem, vmem, _ = specs()
    columns = float(queries.shape[1] * heads)
    grads = jax.ShapeDtypeStruct(queries.shape, BF16)
    return pl.pallas_call(
        lambda *refs: backward_kernel(pairs, 1.0 / math.sqrt(DH), columns, *refs),
        out_shape=(grads, grads)
        + tuple(jax.ShapeDtypeStruct((n * PART, 2 * DH), BF16) for n in SENT),
        in_specs=[smem, smem] + [vmem] * 7,
        out_specs=(vmem,) * (2 + len(SENT)),
        scratch_shapes=[
            pltpu.VMEM(((per_device * count + 1) * BLOCK, 2 * DH), F32),
        ],
        compiler_params=pltpu.CompilerParams(vmem_limit_bytes=14 << 20),
        cost_estimate=pl.CostEstimate(flops=5 * flops, bytes_accessed=32 << 20, transcendentals=0),
        name="backward",
    )(slots, holder, sums, queries, cotangent, gain, attended, weights, held)


def body(queries, keys, values, cotangent, gain, key_blocks, span_order):
    key_width = keys.shape[1]
    heads = lax.axis_size(HEAD)
    gain = gain.reshape(1, queries.shape[1])
    gathered = gather_blocks(jnp.concatenate([keys, values], axis=1))
    slots, source_of, back_of = positions(key_blocks, span_order, queries.shape[0] // BLOCK)
    attended, weights, held, sums = forward(
        heads, slots, source_of, queries, cotangent, gain, gathered
    )
    sums = head_copies(sums)
    output, query_grad, *parts = backward(
        heads, slots, back_of, sums, queries, cotangent, gain, attended, weights, held
    )
    grads = scatter_blocks(*parts).astype(BF16)
    return output, query_grad, grads[:, :key_width], grads[:, key_width:]


def solution(mesh):
    fine = Mesh(mesh.devices.reshape(NZ, 2, 2, 4, 2), CTX + HEAD)
    tok = P(CTX, HEAD)
    return jax.shard_map(
        body,
        mesh=fine,
        in_specs=(tok, tok, tok, tok, P(HEAD), P(), P()),
        out_specs=(tok, tok, tok, tok),
        check_vma=False,
    )
```

profile of v0, /device:TPU:4, one launch (start us, length us, event | category | flops | bytes accessed | tf_op | source)
XLA Modules:
  0.0 235.9 jit_solution(12444729434454630676)
XLA Ops:
  2.3 7.8 %collective-permute-start = (bf16[256,256]{1,0:T(8,128)(2,1)S(1)}, bf16[256,256]{1,0:T(8,128)(2,1)S(1)}, u32[]{:S(2)}, u32[]{:S(2)}) collective-permute-start(bf16[256,256]{1,0:T(8,128)(2,1)S(1)} %constant_dynamic-update-slice_fusion), channel_id=1, source_target_pairs={{0,16},{16,0},{1,17},{17,1},{2,18},{18,2},{3,19},{19,3},{4,20},{20... | collective-permute-start | bytes 393224 | tf_op jit(solution)/shard_map/ppermute | solution.py:43
  10.1 2.9 %collective-permute-done = bf16[256,256]{1,0:T(8,128)(2,1)S(1)} collective-permute-done((bf16[256,256]{1,0:T(8,128)(2,1)S(1)}, bf16[256,256]{1,0:T(8,128)(2,1)S(1)}, u32[]{:S(2)}, u32[]{:S(2)}) %collective-permute-start) | collective-permute-done | bytes 131104 | tf_op jit(solution)/shard_map/ppermute | solution.py:43
  17.0 3.7 %collective-permute-start.3 = (bf16[512,256]{1,0:T(8,128)(2,1)S(1)}, bf16[512,256]{1,0:T(8,128)(2,1)S(1)}, u32[]{:S(2)}, u32[]{:S(2)}) collective-permute-start(bf16[512,256]{1,0:T(8,128)(2,1)S(1)} %collective-permute-done.1.refs_6_), channel_id=1, source_target_pairs={{0,32},{8,488},{32,64},{40,8},{64,96},{72,40},{96,128},{104,72},{1... | collective-permute-start | bytes 786440 | tf_op jit(solution)/shard_map/ppermute | solution.py:35
  20.6 8.1 %collective-permute-done.2.refs_7_ = bf16[512,256]{1,0:T(8,128)(2,1)S(1)} collective-permute-done((bf16[512,256]{1,0:T(8,128)(2,1)S(1)}, bf16[512,256]{1,0:T(8,128)(2,1)S(1)}, u32[]{:S(2)}, u32[]{:S(2)}) %collective-permute-start.2) | collective-permute-done | bytes 262176 | tf_op jit(solution)/shard_map/ppermute | solution.py:35
  33.4 4.7 %collective-permute-done.4.refs_9_ = bf16[512,256]{1,0:T(8,128)(2,1)S(1)} collective-permute-done((bf16[512,256]{1,0:T(8,128)(2,1)S(1)}, bf16[512,256]{1,0:T(8,128)(2,1)S(1)}, u32[]{:S(2)}, u32[]{:S(2)}) %collective-permute-start.4) | collective-permute-done | bytes 262176 | tf_op jit(solution)/shard_map/ppermute | solution.py:35
  43.6 4.0 %collective-permute-done.6.refs_11_ = bf16[512,256]{1,0:T(8,128)(2,1)S(1)} collective-permute-done((bf16[512,256]{1,0:T(8,128)(2,1)S(1)}, bf16[512,256]{1,0:T(8,128)(2,1)S(1)}, u32[]{:S(2)}, u32[]{:S(2)}) %collective-permute-start.6) | collective-permute-done | bytes 262176 | tf_op jit(solution)/shard_map/ppermute | solution.py:35
  54.7 2.4 %collective-permute-done.8.refs_13_ = bf16[512,256]{1,0:T(8,128)(2,1)S(1)} collective-permute-done((bf16[512,256]{1,0:T(8,128)(2,1)S(1)}, bf16[512,256]{1,0:T(8,128)(2,1)S(1)}, u32[]{:S(2)}, u32[]{:S(2)}) %collective-permute-start.8) | collective-permute-done | bytes 262176 | tf_op jit(solution)/shard_map/ppermute | solution.py:35
  62.0 4.5 %collective-permute-done.10.refs_15_ = bf16[512,256]{1,0:T(8,128)(2,1)S(1)} collective-permute-done((bf16[512,256]{1,0:T(8,128)(2,1)S(1)}, bf16[512,256]{1,0:T(8,128)(2,1)S(1)}, u32[]{:S(2)}, u32[]{:S(2)}) %collective-permute-start.10) | collective-permute-done | bytes 262176 | tf_op jit(solution)/shard_map/ppermute | solution.py:35
  74.6 2.5 %collective-permute-start.17 = (bf16[2048,256]{1,0:T(8,128)(2,1)S(1)}, bf16[2048,256]{1,0:T(8,128)(2,1)}, u32[]{:S(2)}, u32[]{:S(2)}) collective-permute-start(bf16[2048,256]{1,0:T(8,128)(2,1)S(1)} %pad_maximum_fusion.1), channel_id=1, source_target_pairs={{0,8},{8,0},{1,9},{9,1},{2,10},{10,2},{3,11},{11,3},{4,12},{12,4},... | collective-permute-start | bytes 3145736 | tf_op jit(solution)/shard_map/ppermute | solution.py:39
  84.3 2.3 collective-permute-start.15
  87.0 5.1 %collective-permute-done.14.refs_19_ = bf16[512,256]{1,0:T(8,128)(2,1)S(1)} collective-permute-done((bf16[512,256]{1,0:T(8,128)(2,1)}, bf16[512,256]{1,0:T(8,128)(2,1)S(1)}, u32[]{:S(2)}, u32[]{:S(2)}) %collective-permute-start.14) | collective-permute-done | bytes 262176 | tf_op jit(solution)/shard_map/ppermute | solution.py:35
  92.1 2.8 %collective-permute-done.15.refs_20_ = bf16[512,256]{1,0:T(8,128)(2,1)S(1)} collective-permute-done((bf16[512,256]{1,0:T(8,128)(2,1)}, bf16[512,256]{1,0:T(8,128)(2,1)S(1)}, u32[]{:S(2)}, u32[]{:S(2)}) %collective-permute-start.15) | collective-permute-done | bytes 262176 | tf_op jit(solution)/shard_map/ppermute | solution.py:35
  101.8 5.4 %collective-permute-done.20.refs_25_ = bf16[512,256]{1,0:T(8,128)(2,1)S(1)} collective-permute-done((bf16[512,256]{1,0:T(8,128)(2,1)S(1)}, bf16[512,256]{1,0:T(8,128)(2,1)S(1)}, u32[]{:S(2)}, u32[]{:S(2)}) %collective-permute-start.20) | collective-permute-done | bytes 262176 | tf_op jit(solution)/shard_map/ppermute | solution.py:35
  107.2 2.9 %collective-permute-done.21.refs_26_ = bf16[512,256]{1,0:T(8,128)(2,1)} collective-permute-done((bf16[512,256]{1,0:T(8,128)(2,1)S(1)}, bf16[512,256]{1,0:T(8,128)(2,1)}, u32[]{:S(2)}, u32[]{:S(2)}) %collective-permute-start.21) | collective-permute-done | bytes 262176 | tf_op jit(solution)/shard_map/ppermute | solution.py:35
  110.2 10.2 %forward.1 = (f32[2,128,512]{2,1,0:T(8,128)S(1)}, f32[2,2688,512]{2,1,0:T(8,128)S(1)}, bf16[5504,256]{1,0:T(8,128)(2,1)S(1)}, f32[8,4,128]{2,1,0:T(4,128)S(1)}) custom-call(s32[2,21]{1,0:T(2,128)S(1)} %compare_select_fusion.7.refs_0_, s32[128]{0:T(128)S(1)} %get-tuple-element.70.refs_1_, bf16[256,512]{1,0:T(8,128)(2,1)S(1)} %copy-done, ...), custom_call_target="tpu_custom_call" | custom-call | flops 1409286144 | bytes 16777216 | tf_op jit(solution)/shard_map/forward/pallas_call | solution.py:328
  120.4 11.1 %all_to_all.5.refs_2_ = f32[8,4,128]{2,1,0:T(4,128)S(1)} all-to-all(f32[8,4,128]{2,1,0:T(4,128)S(1)} %get-tuple-element.37), channel_id=1, replica_groups=mesh['z'=16,'xh'=2,'core'=2,'y'=4,'xl'=2] {'y','xl'}, dimensions={0} | all-to-all | bytes 32768 | tf_op jit(solution)/shard_map/all_to_all | solution.py:88
  131.6 11.3 %backward.1 = (bf16[256,512]{1,0:T(8,128)(2,1)}, bf16[256,512]{1,0:T(8,128)(2,1)}, bf16[8192,256]{1,0:T(8,128)(2,1)S(1)}, bf16[3072,256]{1,0:T(8,128)(2,1)S(1)},...) custom-call(s32[2,21]{1,0:T(2,128)S(1)} %compare_select_fusion.7.ref, ...), custom_call_target="tpu_custom_call" | custom-call | flops 3523215360 | bytes 33554432 | tf_op jit(solution)/shard_map/backward/pallas_call | solution.py:350
  146.7 3.4 %collective-permute-start.29 = (bf16[2048,256]{1,0:T(8,128)(2,1)S(1)}, bf16[2048,256]{1,0:T(8,128)(2,1)S(1)}, u32[]{:S(2)}, u32[]{:S(2)}) collective-permute-start(bf16[2048,256]{1,0:T(8,128)(2,1)S(1)} %get-tuple-element.53), channel_id=1, source_target_pairs={{0,8},{8,0},{1,9},{9,1},{2,10},{10,2},{3,11},{11,3},{4,12},{12,4},... | collective-permute-start | bytes 3145736 | tf_op jit(solution)/shard_map/ppermute | solution.py:39
  150.2 2.6 %collective-permute-start.22 = (bf16[512,256]{1,0:T(8,128)(2,1)S(1)}, bf16[512,256]{1,0:T(8,128)(2,1)S(1)}, u32[]{:S(2)}, u32[]{:S(2)}) collective-permute-start(bf16[512,256]{1,0:T(8,128)(2,1)S(1)} %get-tuple-element.43), channel_id=1, source_target_pairs={{0,32},{8,488},{32,64},{40,8},{64,96},{72,40},{96,128},{104,72},{1... | collective-permute-start | bytes 786440 | tf_op jit(solution)/shard_map/ppermute | solution.py:35
  156.3 2.3 collective-permute-start.34
  159.7 2.5 %collective-permute-start.25 = (bf16[512,256]{1,0:T(8,128)(2,1)S(1)}, bf16[512,256]{1,0:T(8,128)(2,1)S(1)}, u32[]{:S(2)}, u32[]{:S(2)}) collective-permute-start(bf16[512,256]{1,0:T(8,128)(2,1)S(1)} %add_convert_fusion.13), channel_id=1, source_target_pairs={{0,32},{8,488},{32,64},{40,8},{64,96},{72,40},{96,128},{104,72},{1... | collective-permute-start | bytes 786440 | tf_op jit(solution)/shard_map/ppermute | solution.py:35
  165.9 3.3 %collective-permute-done.25 = bf16[512,256]{1,0:T(8,128)(2,1)S(1)} collective-permute-done((bf16[512,256]{1,0:T(8,128)(2,1)S(1)}, bf16[512,256]{1,0:T(8,128)(2,1)S(1)}, u32[]{:S(2)}, u32[]{:S(2)}) %collective-permute-start.25) | collective-permute-done | bytes 262176 | tf_op jit(solution)/shard_map/ppermute | solution.py:35
  175.5 3.3 %collective-permute-done.27 = bf16[512,256]{1,0:T(8,128)(2,1)S(1)} collective-permute-done((bf16[512,256]{1,0:T(8,128)(2,1)S(1)}, bf16[512,256]{1,0:T(8,128)(2,1)S(1)}, u32[]{:S(2)}, u32[]{:S(2)}) %collective-permute-start.27) | collective-permute-done | bytes 262176 | tf_op jit(solution)/shard_map/ppermute | solution.py:35
  180.8 2.2 collective-permute-done.31
  185.1 3.3 %collective-permute-done.30 = bf16[512,256]{1,0:T(8,128)(2,1)S(1)} collective-permute-done((bf16[512,256]{1,0:T(8,128)(2,1)S(1)}, bf16[512,256]{1,0:T(8,128)(2,1)S(1)}, u32[]{:S(2)}, u32[]{:S(2)}) %collective-permute-start.30) | collective-permute-done | bytes 262176 | tf_op jit(solution)/shard_map/ppermute | solution.py:35
  194.7 3.3 %collective-permute-done.32 = bf16[512,256]{1,0:T(8,128)(2,1)S(1)} collective-permute-done((bf16[512,256]{1,0:T(8,128)(2,1)S(1)}, bf16[512,256]{1,0:T(8,128)(2,1)S(1)}, u32[]{:S(2)}, u32[]{:S(2)}) %collective-permute-start.32) | collective-permute-done | bytes 262176 | tf_op jit(solution)/shard_map/ppermute | solution.py:35
  200.0 2.2 collective-permute-done.36
  204.2 3.3 %collective-permute-done.35 = bf16[512,256]{1,0:T(8,128)(2,1)S(1)} collective-permute-done((bf16[512,256]{1,0:T(8,128)(2,1)S(1)}, bf16[512,256]{1,0:T(8,128)(2,1)S(1)}, u32[]{:S(2)}, u32[]{:S(2)}) %collective-permute-start.35) | collective-permute-done | bytes 262176 | tf_op jit(solution)/shard_map/ppermute | solution.py:35
  213.8 3.3 %collective-permute-done.37 = bf16[512,256]{1,0:T(8,128)(2,1)S(1)} collective-permute-done((bf16[512,256]{1,0:T(8,128)(2,1)S(1)}, bf16[512,256]{1,0:T(8,128)(2,1)S(1)}, u32[]{:S(2)}, u32[]{:S(2)}) %collective-permute-start.37) | collective-permute-done | bytes 262176 | tf_op jit(solution)/shard_map/ppermute | solution.py:35
  223.4 3.3 %collective-permute-done.39 = bf16[512,256]{1,0:T(8,128)(2,1)S(1)} collective-permute-done((bf16[512,256]{1,0:T(8,128)(2,1)S(1)}, bf16[512,256]{1,0:T(8,128)(2,1)S(1)}, u32[]{:S(2)}, u32[]{:S(2)}) %collective-permute-start.39) | collective-permute-done | bytes 262176 | tf_op jit(solution)/shard_map/ppermute | solution.py:35
  226.8 2.5 %collective-permute-start.42 = (bf16[256,256]{1,0:T(8,128)(2,1)S(1)}, bf16[256,256]{1,0:T(8,128)(2,1)S(1)}, u32[]{:S(2)}, u32[]{:S(2)}) collective-permute-start(bf16[256,256]{1,0:T(8,128)(2,1)S(1)} %slice.182), channel_id=1, source_target_pairs={{0,16},{16,0},{1,17},{17,1},{2,18},{18,2},{3,19},{19,3},{4,20},{20... | collective-permute-start | bytes 393224 | tf_op jit(solution)/shard_map/ppermute | solution.py:83
  229.3 5.9 %collective-permute-done.42 = bf16[256,256]{1,0:T(8,128)(2,1)S(1)} collective-permute-done((bf16[256,256]{1,0:T(8,128)(2,1)S(1)}, bf16[256,256]{1,0:T(8,128)(2,1)S(1)}, u32[]{:S(2)}, u32[]{:S(2)}) %collective-permute-start.42) | collective-permute-done | bytes 131104 | tf_op jit(solution)/shard_map/ppermute | solution.py:83
  (138 shorter events, 95.9 us)
Async XLA Ops:
  2.3 10.7 %collective-permute-start = (bf16[256,256]{1,0:T(8,128)(2,1)S(1)}, bf16[256,256]{1,0:T(8,128)(2,1)S(1)}, u32[]{:S(2)}, u32[]{:S(2)}) collective-permute-start(bf16[256,256]{1,0:T(8,128)(2,1)S(1)} %constant_dynamic-update-slice_fusion), channel_id=1, source_target_pairs={{0,16},{16,0},{1,17},{17,1},{2,18},{18,2},{3,19},{19,3},{4,20},{20... | collective-permute-start | bytes 393224 | tf_op jit(solution)/shard_map/ppermute | solution.py:43
  15.0 13.7 %collective-permute-start.2 = (bf16[512,256]{1,0:T(8,128)(2,1)S(1)}, bf16[512,256]{1,0:T(8,128)(2,1)S(1)}, u32[]{:S(2)}, u32[]{:S(2)}) collective-permute-start(bf16[512,256]{1,0:T(8,128)(2,1)S(1)} %pad_maximum_fusion.4.refs_5_), channel_id=1, source_target_pairs={{0,32},{8,488},{32,64},{40,8},{64,96},{72,40},{96,128},{104,72},{1... | collective-permute-start | bytes 786440 | tf_op jit(solution)/shard_map/ppermute | solution.py:35
  17.0 14.5 %collective-permute-start.3 = (bf16[512,256]{1,0:T(8,128)(2,1)S(1)}, bf16[512,256]{1,0:T(8,128)(2,1)S(1)}, u32[]{:S(2)}, u32[]{:S(2)}) collective-permute-start(bf16[512,256]{1,0:T(8,128)(2,1)S(1)} %collective-permute-done.1.refs_6_), channel_id=1, source_target_pairs={{0,32},{8,488},{32,64},{40,8},{64,96},{72,40},{96,128},{104,72},{1... | collective-permute-start | bytes 786440 | tf_op jit(solution)/shard_map/ppermute | solution.py:35
  59.9 9.6 %collective-permute-start.11 = (bf16[512,256]{1,0:T(8,128)(2,1)S(1)}, bf16[512,256]{1,0:T(8,128)(2,1)}, u32[]{:S(2)}, u32[]{:S(2)}) collective-permute-start(bf16[512,256]{1,0:T(8,128)(2,1)S(1)} %collective-permute-done.9.refs_14_), channel_id=1, source_target_pairs={{0,32},{8,488},{32,64},{40,8},{64,96},{72,40},{96,128},{104,72},{1... | collective-permute-start | bytes 786440 | tf_op jit(solution)/shard_map/ppermute | solution.py:35
  66.6 10.5 %collective-permute-start.12 = (bf16[512,256]{1,0:T(8,128)(2,1)S(1)}, bf16[512,256]{1,0:T(8,128)(2,1)S(1)}, u32[]{:S(2)}, u32[]{:S(2)}) collective-permute-start(bf16[512,256]{1,0:T(8,128)(2,1)S(1)} %collective-permute-done.10.refs_15_), channel_id=1, source_target_pairs={{0,32},{8,488},{32,64},{40,8},{64,96},{72,40},{96,128},{104,72},{1... | collective-permute-start | bytes 786440 | tf_op jit(solution)/shard_map/ppermute | solution.py:35
  69.5 9.7 %collective-permute-start.13 = (bf16[512,256]{1,0:T(8,128)(2,1)}, bf16[512,256]{1,0:T(8,128)(2,1)S(1)}, u32[]{:S(2)}, u32[]{:S(2)}) collective-permute-start(bf16[512,256]{1,0:T(8,128)(2,1)} %collective-permute-done.11.refs_16_), channel_id=1, source_target_pairs={{0,32},{8,488},{32,64},{40,8},{64,96},{72,40},{96,128},{104,72},{1... | collective-permute-start | bytes 786440 | tf_op jit(solution)/shard_map/ppermute | solution.py:35
  72.4 27.2 %collective-permute-start.16 = (bf16[2048,256]{1,0:T(8,128)(2,1)}, bf16[2048,256]{1,0:T(8,128)(2,1)}, u32[]{:S(2)}, u32[]{:S(2)}) collective-permute-start(bf16[2048,256]{1,0:T(8,128)(2,1)} %pad_maximum_fusion), channel_id=1, source_target_pairs={{0,8},{8,0},{1,9},{9,1},{2,10},{10,2},{3,11},{11,3},{4,12},{12,4},... | collective-permute-start | bytes 3145736 | tf_op jit(solution)/shard_map/ppermute | solution.py:39
  74.6 35.6 %collective-permute-start.17 = (bf16[2048,256]{1,0:T(8,128)(2,1)S(1)}, bf16[2048,256]{1,0:T(8,128)(2,1)}, u32[]{:S(2)}, u32[]{:S(2)}) collective-permute-start(bf16[2048,256]{1,0:T(8,128)(2,1)S(1)} %pad_maximum_fusion.1), channel_id=1, source_target_pairs={{0,8},{8,0},{1,9},{9,1},{2,10},{10,2},{3,11},{11,3},{4,12},{12,4},... | collective-permute-start | bytes 3145736 | tf_op jit(solution)/shard_map/ppermute | solution.py:39
  80.3 29.9 %collective-permute-start.18 = (bf16[2048,256]{1,0:T(8,128)(2,1)S(1)}, bf16[2048,256]{1,0:T(8,128)(2,1)}, u32[]{:S(2)}, u32[]{:S(2)}) collective-permute-start(bf16[2048,256]{1,0:T(8,128)(2,1)S(1)} %pad_maximum_fusion.2), channel_id=1, source_target_pairs={{0,8},{8,0},{1,9},{9,1},{2,10},{10,2},{3,11},{11,3},{4,12},{12,4},... | collective-permute-start | bytes 3145736 | tf_op jit(solution)/shard_map/ppermute | solution.py:39
  82.4 9.7 %collective-permute-start.14 = (bf16[512,256]{1,0:T(8,128)(2,1)}, bf16[512,256]{1,0:T(8,128)(2,1)S(1)}, u32[]{:S(2)}, u32[]{:S(2)}) collective-permute-start(bf16[512,256]{1,0:T(8,128)(2,1)} %copy-done.15), channel_id=1, source_target_pairs={{0,32},{8,488},{32,64},{40,8},{64,96},{72,40},{96,128},{104,72},{1... | collective-permute-start | bytes 786440 | tf_op jit(solution)/shard_map/ppermute | solution.py:35
  84.3 10.6 %collective-permute-start.15 = (bf16[512,256]{1,0:T(8,128)(2,1)}, bf16[512,256]{1,0:T(8,128)(2,1)S(1)}, u32[]{:S(2)}, u32[]{:S(2)}) collective-permute-start(bf16[512,256]{1,0:T(8,128)(2,1)} %copy-done.16), channel_id=1, source_target_pairs={{0,32},{8,488},{32,64},{40,8},{64,96},{72,40},{96,128},{104,72},{1... | collective-permute-start | bytes 786440 | tf_op jit(solution)/shard_map/ppermute | solution.py:35
  95.8 14.3 %collective-permute-start.19 = (bf16[1024,256]{1,0:T(8,128)(2,1)}, bf16[1024,256]{1,0:T(8,128)(2,1)}, u32[]{:S(2)}, u32[]{:S(2)}) collective-permute-start(bf16[1024,256]{1,0:T(8,128)(2,1)} %pad_maximum_fusion.3), channel_id=1, source_target_pairs={{0,8},{8,0},{1,9},{9,1},{2,10},{10,2},{3,11},{11,3},{4,12},{12,4},... | collective-permute-start | bytes 1572872 | tf_op jit(solution)/shard_map/ppermute | solution.py:39
  97.7 9.5 %collective-permute-start.20 = (bf16[512,256]{1,0:T(8,128)(2,1)S(1)}, bf16[512,256]{1,0:T(8,128)(2,1)S(1)}, u32[]{:S(2)}, u32[]{:S(2)}) collective-permute-start(bf16[512,256]{1,0:T(8,128)(2,1)S(1)} %collective-permute-done.14.refs_19_), channel_id=1, source_target_pairs={{0,32},{8,488},{32,64},{40,8},{64,96},{72,40},{96,128},{104,72},{1... | collective-permute-start | bytes 786440 | tf_op jit(solution)/shard_map/ppermute | solution.py:35
  99.7 10.5 %collective-permute-start.21 = (bf16[512,256]{1,0:T(8,128)(2,1)S(1)}, bf16[512,256]{1,0:T(8,128)(2,1)}, u32[]{:S(2)}, u32[]{:S(2)}) collective-permute-start(bf16[512,256]{1,0:T(8,128)(2,1)S(1)} %collective-permute-done.15.refs_20_), channel_id=1, source_target_pairs={{0,32},{8,488},{32,64},{40,8},{64,96},{72,40},{96,128},{104,72},{1... | collective-permute-start | bytes 786440 | tf_op jit(solution)/shard_map/ppermute | solution.py:35
  142.9 11.4 %collective-permute-start.24 = (bf16[2048,256]{1,0:T(8,128)(2,1)S(1)}, bf16[2048,256]{1,0:T(8,128)(2,1)S(1)}, u32[]{:S(2)}, u32[]{:S(2)}) collective-permute-start(bf16[2048,256]{1,0:T(8,128)(2,1)S(1)} %get-tuple-element.46), channel_id=1, source_target_pairs={{0,8},{8,0},{1,9},{9,1},{2,10},{10,2},{3,11},{11,3},{4,12},{12,4},... | collective-permute-start | bytes 3145736 | tf_op jit(solution)/shard_map/ppermute | solution.py:39
  144.8 9.5 %collective-permute-start.23 = (bf16[512,256]{1,0:T(8,128)(2,1)S(1)}, bf16[512,256]{1,0:T(8,128)(2,1)S(1)}, u32[]{:S(2)}, u32[]{:S(2)}) collective-permute-start(bf16[512,256]{1,0:T(8,128)(2,1)S(1)} %get-tuple-element.44), channel_id=1, source_target_pairs={{0,32},{8,488},{32,64},{40,8},{64,96},{72,40},{96,128},{104,72},{1... | collective-permute-start | bytes 786440 | tf_op jit(solution)/shard_map/ppermute | solution.py:35
  146.7 24.5 %collective-permute-start.29 = (bf16[2048,256]{1,0:T(8,128)(2,1)S(1)}, bf16[2048,256]{1,0:T(8,128)(2,1)S(1)}, u32[]{:S(2)}, u32[]{:S(2)}) collective-permute-start(bf16[2048,256]{1,0:T(8,128)(2,1)S(1)} %get-tuple-element.53), channel_id=1, source_target_pairs={{0,8},{8,0},{1,9},{9,1},{2,10},{10,2},{3,11},{11,3},{4,12},{12,4},... | collective-permute-start | bytes 3145736 | tf_op jit(solution)/shard_map/ppermute | solution.py:39
  150.2 9.5 %collective-permute-start.22 = (bf16[512,256]{1,0:T(8,128)(2,1)S(1)}, bf16[512,256]{1,0:T(8,128)(2,1)S(1)}, u32[]{:S(2)}, u32[]{:S(2)}) collective-permute-start(bf16[512,256]{1,0:T(8,128)(2,1)S(1)} %get-tuple-element.43), channel_id=1, source_target_pairs={{0,32},{8,488},{32,64},{40,8},{64,96},{72,40},{96,128},{104,72},{1... | collective-permute-start | bytes 786440 | tf_op jit(solution)/shard_map/ppermute | solution.py:35
  154.4 9.5 %collective-permute-start.26 = (bf16[512,256]{1,0:T(8,128)(2,1)S(1)}, bf16[512,256]{1,0:T(8,128)(2,1)S(1)}, u32[]{:S(2)}, u32[]{:S(2)}) collective-permute-start(bf16[512,256]{1,0:T(8,128)(2,1)S(1)} %add_convert_fusion.14), channel_id=1, source_target_pairs={{0,32},{8,488},{32,64},{40,8},{64,96},{72,40},{96,128},{104,72},{1... | collective-permute-start | bytes 786440 | tf_op jit(solution)/shard_map/ppermute | solution.py:35
  156.3 34.1 %collective-permute-start.34 = (bf16[3072,256]{1,0:T(8,128)(2,1)S(1)}, bf16[3072,256]{1,0:T(8,128)(2,1)S(1)}, u32[]{:S(2)}, u32[]{:S(2)}) collective-permute-start(bf16[3072,256]{1,0:T(8,128)(2,1)S(1)} %get-tuple-element.60), channel_id=1, source_target_pairs={{0,8},{8,0},{1,9},{9,1},{2,10},{10,2},{3,11},{11,3},{4,12},{12,4},... | collective-permute-start | bytes 4718600 | tf_op jit(solution)/shard_map/ppermute | solution.py:39
  159.7 9.5 %collective-permute-start.25 = (bf16[512,256]{1,0:T(8,128)(2,1)S(1)}, bf16[512,256]{1,0:T(8,128)(2,1)S(1)}, u32[]{:S(2)}, u32[]{:S(2)}) collective-permute-start(bf16[512,256]{1,0:T(8,128)(2,1)S(1)} %add_convert_fusion.13), channel_id=1, source_target_pairs={{0,32},{8,488},{32,64},{40,8},{64,96},{72,40},{96,128},{104,72},{1... | collective-permute-start | bytes 786440 | tf_op jit(solution)/shard_map/ppermute | solution.py:35
  164.0 9.5 %collective-permute-start.28 = (bf16[512,256]{1,0:T(8,128)(2,1)S(1)}, bf16[512,256]{1,0:T(8,128)(2,1)S(1)}, u32[]{:S(2)}, u32[]{:S(2)}) collective-permute-start(bf16[512,256]{1,0:T(8,128)(2,1)S(1)} %add_convert_fusion.12), channel_id=1, source_target_pairs={{0,32},{8,488},{32,64},{40,8},{64,96},{72,40},{96,128},{104,72},{1... | collective-permute-start | bytes 786440 | tf_op jit(solution)/shard_map/ppermute | solution.py:35
  169.3 9.5 %collective-permute-start.27 = (bf16[512,256]{1,0:T(8,128)(2,1)S(1)}, bf16[512,256]{1,0:T(8,128)(2,1)S(1)}, u32[]{:S(2)}, u32[]{:S(2)}) collective-permute-start(bf16[512,256]{1,0:T(8,128)(2,1)S(1)} %add_convert_fusion.11), channel_id=1, source_target_pairs={{0,32},{8,488},{32,64},{40,8},{64,96},{72,40},{96,128},{104,72},{1... | collective-permute-start | bytes 786440 | tf_op jit(solution)/shard_map/ppermute | solution.py:35
  173.6 9.5 %collective-permute-start.31 = (bf16[512,256]{1,0:T(8,128)(2,1)S(1)}, bf16[512,256]{1,0:T(8,128)(2,1)S(1)}, u32[]{:S(2)}, u32[]{:S(2)}) collective-permute-start(bf16[512,256]{1,0:T(8,128)(2,1)S(1)} %add_convert_fusion.10), channel_id=1, source_target_pairs={{0,32},{8,488},{32,64},{40,8},{64,96},{72,40},{96,128},{104,72},{1... | collective-permute-start | bytes 786440 | tf_op jit(solution)/shard_map/ppermute | solution.py:35
  178.9 9.5 %collective-permute-start.30 = (bf16[512,256]{1,0:T(8,128)(2,1)S(1)}, bf16[512,256]{1,0:T(8,128)(2,1)S(1)}, u32[]{:S(2)}, u32[]{:S(2)}) collective-permute-start(bf16[512,256]{1,0:T(8,128)(2,1)S(1)} %add_convert_fusion.9), channel_id=1, source_target_pairs={{0,32},{8,488},{32,64},{40,8},{64,96},{72,40},{96,128},{104,72},{1... | collective-permute-start | bytes 786440 | tf_op jit(solution)/shard_map/ppermute | solution.py:35
  183.1 9.5 %collective-permute-start.33 = (bf16[512,256]{1,0:T(8,128)(2,1)S(1)}, bf16[512,256]{1,0:T(8,128)(2,1)S(1)}, u32[]{:S(2)}, u32[]{:S(2)}) collective-permute-start(bf16[512,256]{1,0:T(8,128)(2,1)S(1)} %add_convert_fusion.8), channel_id=1, source_target_pairs={{0,32},{8,488},{32,64},{40,8},{64,96},{72,40},{96,128},{104,72},{1... | collective-permute-start | bytes 786440 | tf_op jit(solution)/shard_map/ppermute | solution.py:35
  188.5 9.5 %collective-permute-start.32 = (bf16[512,256]{1,0:T(8,128)(2,1)S(1)}, bf16[512,256]{1,0:T(8,128)(2,1)S(1)}, u32[]{:S(2)}, u32[]{:S(2)}) collective-permute-start(bf16[512,256]{1,0:T(8,128)(2,1)S(1)} %add_convert_fusion.7), channel_id=1, source_target_pairs={{0,32},{8,488},{32,64},{40,8},{64,96},{72,40},{96,128},{104,72},{1... | collective-permute-start | bytes 786440 | tf_op jit(solution)/shard_map/ppermute | solution.py:35
  192.7 9.5 %collective-permute-start.36 = (bf16[512,256]{1,0:T(8,128)(2,1)S(1)}, bf16[512,256]{1,0:T(8,128)(2,1)S(1)}, u32[]{:S(2)}, u32[]{:S(2)}) collective-permute-start(bf16[512,256]{1,0:T(8,128)(2,1)S(1)} %add_convert_fusion.6), channel_id=1, source_target_pairs={{0,32},{8,488},{32,64},{40,8},{64,96},{72,40},{96,128},{104,72},{1... | collective-permute-start | bytes 786440 | tf_op jit(solution)/shard_map/ppermute | solution.py:35
  198.1 9.5 %collective-permute-start.35 = (bf16[512,256]{1,0:T(8,128)(2,1)S(1)}, bf16[512,256]{1,0:T(8,128)(2,1)S(1)}, u32[]{:S(2)}, u32[]{:S(2)}) collective-permute-start(bf16[512,256]{1,0:T(8,128)(2,1)S(1)} %add_convert_fusion.5), channel_id=1, source_target_pairs={{0,32},{8,488},{32,64},{40,8},{64,96},{72,40},{96,128},{104,72},{1... | collective-permute-start | bytes 786440 | tf_op jit(solution)/shard_map/ppermute | solution.py:35
  202.3 9.5 %collective-permute-start.38 = (bf16[512,256]{1,0:T(8,128)(2,1)S(1)}, bf16[512,256]{1,0:T(8,128)(2,1)S(1)}, u32[]{:S(2)}, u32[]{:S(2)}) collective-permute-start(bf16[512,256]{1,0:T(8,128)(2,1)S(1)} %add_convert_fusion.4), channel_id=1, source_target_pairs={{0,32},{8,488},{32,64},{40,8},{64,96},{72,40},{96,128},{104,72},{1... | collective-permute-start | bytes 786440 | tf_op jit(solution)/shard_map/ppermute | solution.py:35
  207.7 9.5 %collective-permute-start.37 = (bf16[512,256]{1,0:T(8,128)(2,1)S(1)}, bf16[512,256]{1,0:T(8,128)(2,1)S(1)}, u32[]{:S(2)}, u32[]{:S(2)}) collective-permute-start(bf16[512,256]{1,0:T(8,128)(2,1)S(1)} %add_convert_fusion.3), channel_id=1, source_target_pairs={{0,32},{8,488},{32,64},{40,8},{64,96},{72,40},{96,128},{104,72},{1... | collective-permute-start | bytes 786440 | tf_op jit(solution)/shard_map/ppermute | solution.py:35
  211.9 9.5 %collective-permute-start.40 = (bf16[512,256]{1,0:T(8,128)(2,1)S(1)}, bf16[512,256]{1,0:T(8,128)(2,1)S(1)}, u32[]{:S(2)}, u32[]{:S(2)}) collective-permute-start(bf16[512,256]{1,0:T(8,128)(2,1)S(1)} %add_convert_fusion.2), channel_id=1, source_target_pairs={{0,32},{8,488},{32,64},{40,8},{64,96},{72,40},{96,128},{104,72},{1... | collective-permute-start | bytes 786440 | tf_op jit(solution)/shard_map/ppermute | solution.py:35
  (30 other events, 571.5 us)
where the time goes:
time: 237 us; the launch traced here: 236 us
  waiting for transfers between devices  95.9 us (40%)
  starting transfers between devices  94.7 us (40%)
  Pallas kernels  21.5 us (9%)
  blocking collectives  11.1 us (5%)
  other arithmetic  7.64 us (3%)
  local copies, waits for them, and re-layouts  3.63 us (2%)
    ppermute x32, waiting for transfers between devices, ring(): return lax.ppermute(x, RING, ring_pairs())  87.1 us
    ppermute x32, starting transfers between devices, ring(): return lax.ppermute(x, RING, ring_pairs())  64.7 us
    ppermute x9, starting transfers between devices, swap(): return lax.ppermute(x, 'core', SWAP)  19.7 us
    pallas_call x1, Pallas kernels, backward(): pl.pallas_call(lambda *refs: backward_kernel(pairs, 1.0 / math.sqrt(DH),...  11.3 us
    all_to_all x1, blocking collectives, head_copies(): return lax.all_to_all(x, HEAD, 0, 0, tiled=True)  11.1 us
    pallas_call x1, Pallas kernels, forward(): pl.pallas_call(lambda *refs: forward_kernel(pairs, 1.0 / math.sqrt(DH), m...  10.2 us
    ppermute x1, starting transfers between devices, gather_blocks(): pair = jnp.concatenate([kv, lax.ppermute(kv, 'xh', SWAP)], axis=0)  7.76 us
    ppermute x1, waiting for transfers between devices, scatter_blocks(): mate = lax.ppermute(keep[rows:].astype(BF16), 'xh', SWAP)  5.88 us
  transfers between devices with their start and end apart: 43, of which 33 were waited for; matrix products, arithmetic and copies ran while one was open for 4% of the time, Pallas kernels for 0%

commit v1 on v0

--- a/solution.py
+++ b/solution.py
@@ -76,12 +76,14 @@
         other, later_mine, later_theirs = lax.optimization_barrier((other, mine, theirs))
         own = ring(own)
         own = total(own, part_of(later_mine, 2 * s), part_of(later_theirs, i + 1)).astype(BF16)
+    rows = PART // 2
     other = total(ring(other), part_of(mine, 1)).astype(BF16)
-    own = ring(own)
-    keep = total(own, part_of(mine, 0), swap(other))
-    rows = PART // 2
-    mate = lax.ppermute(keep[rows:].astype(BF16), "xh", SWAP)
-    return keep[:rows] + mate.astype(F32)
+    other, mine = lax.optimization_barrier((other, mine))
+    across = lax.ppermute(other[rows:], ("xh", "core"), [(i, 3 - i) for i in range(4)])
+    near_core = swap(other[:rows])
+    own = total(ring(own), part_of(mine, 0))
+    mate = lax.ppermute(own[rows:].astype(BF16), "xh", SWAP)
+    return total(own[:rows], near_core, across, mate)
 
 
 def head_copies(x):
@@ -237,21 +239,23 @@
             )
 
 
+def row_terms(q, columns, sums):
+    squares = jnp.sum(sums[:, 2 * q, :], axis=0, keepdims=True)
+    crossed = jnp.sum(sums[:, 2 * q + 1, :], axis=0, keepdims=True)
+    return lax.rsqrt(squares / columns + 1e-6), crossed / columns
+
+
 def backward_kernel(
     pairs, scale, columns, slots, holder, sums, queries, cotangent, gain, attended, weights, held, *rest
 ):
-    m = len(SENT)
-    output, query_grad = rest[:2]
-    parts = rest[2 : m + 2]
-    acc = rest[m + 2]
+    scores, parts, acc = rest[0], rest[1:-1], rest[-1]
     per_device, count = slots.shape
     group = queries.shape[1] // DH
     for part in parts:
         part[...] = jnp.zeros(part.shape, BF16)
     grads_t, grads, stacked = [], [], []
     for q in range(per_device):
-        inverse = lax.rsqrt(jnp.sum(sums[:, 2 * q, :], axis=0, keepdims=True) / columns + 1e-6)
-        inner = jnp.sum(sums[:, 2 * q + 1, :], axis=0, keepdims=True) / columns
+        inverse, inner = row_terms(q, columns, sums)
         back = inverse * inverse * inner
         grad_t, grad = [], []
         for h, x in enumerate(heads_of(cotangent, q, group)):
@@ -261,19 +265,17 @@
             low = inverse * (grad_in - att * back)
             grad_t.append(low.astype(BF16))
             grad.append(low.T.astype(BF16))
-            output[pl.ds(q * BLOCK, BLOCK), h * DH : (h + 1) * DH] = (
-                (att * inverse).T * gain_h
-            ).astype(BF16)
         grads_t.append(jnp.concatenate(grad_t, axis=1))
         grads.append(jnp.concatenate(grad, axis=0))
         stacked.append(jnp.concatenate(heads_of(queries, q, group), axis=0))
 
-    def pair_grads(q, both, weight):
-        low = weight.astype(BF16)
+    def pair_grads(q, both, span):
+        weight = weights[q, span, :]
         grad_weight = dot(both[:, DH:], grads_t[q])
         grad_score = (grad_weight * (weight * (1.0 - weight))).astype(BF16)
-        part = jnp.concatenate([dot(grad_score, stacked[q]) * scale, dot(low, grads[q])], axis=1)
-        return contract_first(both[:, :DH], grad_score), part
+        scores[q, span, :] = grad_score
+        low = weight.astype(BF16)
+        return jnp.concatenate([dot(grad_score, stacked[q]) * scale, dot(low, grads[q])], axis=1)
 
     def keep_part(q, j, part):
         slot = slots[q, j]
@@ -283,24 +285,15 @@
         acc[rows_of(slot), :] = part
 
     for q in range(per_device):
-        own = held[rows_of(slots[q, 0]), :]
-        query_part, part = pair_grads(q, own, weights[q, :BLOCK, :])
-        keep_part(q, 0, part)
-
-        def step(i, query_part):
-            two = jnp.concatenate(
-                [held[rows_of(slots[q, 1 + 2 * i]), :], held[rows_of(slots[q, 2 + 2 * i]), :]], axis=0
-            )
-            more, part = pair_grads(q, two, weights[q, pl.ds(*steps_at(i + 1)), :])
+        keep_part(q, 0, pair_grads(q, held[rows_of(slots[q, 0]), :], pl.ds(0, BLOCK)))
+
+        def step(i, carry):
+            part = pair_grads(q, pair_of(held, slots, q, i), pl.ds(*steps_at(i + 1)))
             keep_part(q, 1 + 2 * i, part[:BLOCK])
             keep_part(q, 2 + 2 * i, part[BLOCK:])
-            return query_part + more
-
-        query_part = lax.fori_loop(0, pairs, step, query_part, unroll=True)
-        for h in range(group):
-            query_grad[pl.ds(q * BLOCK, BLOCK), h * DH : (h + 1) * DH] = (
-                query_part[:, h * BLOCK : (h + 1) * BLOCK].T * scale
-            ).astype(BF16)
+            return carry
+
+        lax.fori_loop(0, pairs, step, 0, unroll=True)
 
     def hand_over(k, i, at):
         @pl.when(holder[at] >= 0)
@@ -308,6 +301,37 @@
             parts[k][rows_of(i), :] = acc[rows_of(holder[at]), :].astype(BF16)
 
     each_block(SENT, hand_over)
+
+
+def pair_of(held, slots, q, i):
+    return jnp.concatenate(
+        [held[rows_of(slots[q, 1 + 2 * i]), :], held[rows_of(slots[q, 2 + 2 * i]), :]], axis=0
+    )
+
+
+def finish_kernel(
+    pairs, scale, columns, slots, sums, gain, attended, scores, held, output, query_grad
+):
+    per_device = slots.shape[0]
+    group = output.shape[1] // DH
+    for q in range(per_device):
+        rows = pl.ds(q * BLOCK, BLOCK)
+        inverse, _ = row_terms(q, columns, sums)
+        for h in range(group):
+            span = slice(h * DH, (h + 1) * DH)
+            att = attended[q, :, h * BLOCK : (h + 1) * BLOCK]
+            output[rows, span] = ((att * inverse).T * gain[:, span]).astype(BF16)
+        grad = contract_first(held[rows_of(slots[q, 0]), :DH], scores[q, :BLOCK, :])
+
+        def step(i, grad):
+            two = pair_of(held, slots, q, i)[:, :DH]
+            return grad + contract_first(two, scores[q, pl.ds(*steps_at(i + 1)), :])
+
+        grad = lax.fori_loop(0, pairs, step, grad, unroll=True)
+        for h in range(group):
+            query_grad[rows, h * DH : (h + 1) * DH] = (
+                grad[:, h * BLOCK : (h + 1) * BLOCK].T * scale
+            ).astype(BF16)
 
 
 def specs():
@@ -343,23 +367,37 @@
 
 
 def backward(heads, slots, holder, sums, queries, cotangent, gain, attended, weights, held):
-    per_device, count, pairs, _, flops = sizes(queries, slots)
+    per_device, count, pairs, wide, flops = sizes(queries, slots)
     smem, vmem, _ = specs()
     columns = float(queries.shape[1] * heads)
-    grads = jax.ShapeDtypeStruct(queries.shape, BF16)
     return pl.pallas_call(
         lambda *refs: backward_kernel(pairs, 1.0 / math.sqrt(DH), columns, *refs),
-        out_shape=(grads, grads)
+        out_shape=(jax.ShapeDtypeStruct((per_device, count * BLOCK, wide), BF16),)
         + tuple(jax.ShapeDtypeStruct((n * PART, 2 * DH), BF16) for n in SENT),
         in_specs=[smem, smem] + [vmem] * 7,
-        out_specs=(vmem,) * (2 + len(SENT)),
-        scratch_shapes=[
-            pltpu.VMEM(((per_device * count + 1) * BLOCK, 2 * DH), F32),
-        ],
+        out_specs=(vmem,) * (1 + len(SENT)),
+        scratch_shapes=[pltpu.VMEM(((per_device * count + 1) * BLOCK, 2 * DH), F32)],
         compiler_params=pltpu.CompilerParams(vmem_limit_bytes=14 << 20),
-        cost_estimate=pl.CostEstimate(flops=5 * flops, bytes_accessed=32 << 20, transcendentals=0),
+        cost_estimate=pl.CostEstimate(flops=3 * flops, bytes_accessed=32 << 20, transcendentals=0),
         name="backward",
     )(slots, holder, sums, queries, cotangent, gain, attended, weights, held)
+
+
+def finish(heads, slots, sums, gain, attended, scores, held):
+    per_device, count, pairs, wide, _ = sizes(gain, slots)
+    smem, vmem, _ = specs()
+    width = gain.shape[1]
+    grads = jax.ShapeDtypeStruct((per_device * BLOCK, width), BF16)
+    flops = 2 * count * per_device * wide * BLOCK * DH
+    return pl.pallas_call(
+        lambda *refs: finish_kernel(pairs, 1.0 / math.sqrt(DH), float(width * heads), *refs),
+        out_shape=(grads, grads),
+        in_specs=[smem] + [vmem] * 5,
+        out_specs=(vmem, vmem),
+        compiler_params=pltpu.CompilerParams(vmem_limit_bytes=8 << 20),
+        cost_estimate=pl.CostEstimate(flops=flops, bytes_accessed=8 << 20, transcendentals=0),
+        name="finish",
+    )(slots, sums, gain, attended, scores, held)
 
 
 def body(queries, keys, values, cotangent, gain, key_blocks, span_order):
@@ -372,10 +410,11 @@
         heads, slots, source_of, queries, cotangent, gain, gathered
     )
     sums = head_copies(sums)
-    output, query_grad, *parts = backward(
+    scores, *parts = backward(
         heads, slots, back_of, sums, queries, cotangent, gain, attended, weights, held
     )
     grads = scatter_blocks(*parts).astype(BF16)
+    output, query_grad = finish(heads, slots, sums, gain, attended, scores, held)
     return output, query_grad, grads[:, :key_width], grads[:, key_width:]
 
 

time: 237 us -> 244 us (1.030)
  the two profiles are of different devices: /device:TPU:4 before, /device:TPU:1 now
where the time goes in v1:
time: 244 us; the launch traced here: 243 us
  starting transfers between devices  172 us (70%)
  waiting for transfers between devices  25.4 us (10%)
  Pallas kernels  22.6 us (9%)
  blocking collectives  9.98 us (4%)
  other arithmetic  7.78 us (3%)
  local copies, waits for them, and re-layouts  3.65 us (1%)
    ppermute x32, starting transfers between devices, ring(): return lax.ppermute(x, RING, ring_pairs())  115 us
    ppermute x9, starting transfers between devices, swap(): return lax.ppermute(x, 'core', SWAP)  45 us
    ppermute x32, waiting for transfers between devices, ring(): return lax.ppermute(x, RING, ring_pairs())  19 us
    pallas_call x1, Pallas kernels, forward(): pl.pallas_call(lambda *refs: forward_kernel(pairs, 1.0 / math.sqrt(DH), m...  10.7 us
    all_to_all x1, blocking collectives, head_copies(): return lax.all_to_all(x, HEAD, 0, 0, tiled=True)  9.98 us
    pallas_call x1, Pallas kernels, backward(): pl.pallas_call(lambda *refs: backward_kernel(pairs, 1.0 / math.sqrt(DH),...  9.62 us
    ppermute x1, starting transfers between devices, gather_blocks(): pair = jnp.concatenate([kv, lax.ppermute(kv, 'xh', SWAP)], axis=0)  5.47 us
  transfers between devices with their start and end apart: 44, of which 16 were waited for; matrix products, arithmetic and copies ran while one was open for 4% of the time, Pallas kernels for 1%

profile of v1, /device:TPU:1, one launch (start us, length us, event | category | flops | bytes accessed | tf_op | source)
XLA Modules:
  0.0 242.8 jit_solution(9981570452794734505)
XLA Ops:
  2.3 5.5 %collective-permute-start = (bf16[256,256]{1,0:T(8,128)(2,1)S(1)}, bf16[256,256]{1,0:T(8,128)(2,1)S(1)}, u32[]{:S(2)}, u32[]{:S(2)}) collective-permute-start(bf16[256,256]{1,0:T(8,128)(2,1)S(1)} %constant_dynamic-update-slice_fusion), channel_id=1, source_target_pairs={{0,16},{16,0},{1,17},{17,1},{2,18},{18,2},{3,19},{19,3},{4,20},{20... | collective-permute-start | bytes 393224 | tf_op jit(solution)/shard_map/ppermute | solution.py:43
  10.2 9.3 %collective-permute-start.1 = (bf16[512,256]{1,0:T(8,128)(2,1)S(1)}, bf16[512,256]{1,0:T(8,128)(2,1)S(1)}, u32[]{:S(2)}, u32[]{:S(2)}) collective-permute-start(bf16[512,256]{1,0:T(8,128)(2,1)S(1)} %pad_maximum_fusion.4.refs_5_), channel_id=1, source_target_pairs={{0,8},{8,0},{1,9},{9,1},{2,10},{10,2},{3,11},{11,3},{4,12},{12,4},... | collective-permute-start | bytes 786440 | tf_op jit(solution)/shard_map/ppermute | solution.py:39
  19.5 6.0 %collective-permute-start.2 = (bf16[512,256]{1,0:T(8,128)(2,1)S(1)}, bf16[512,256]{1,0:T(8,128)(2,1)S(1)}, u32[]{:S(2)}, u32[]{:S(2)}) collective-permute-start(bf16[512,256]{1,0:T(8,128)(2,1)S(1)} %pad_maximum_fusion.4.refs_5_), channel_id=1, source_target_pairs={{0,32},{8,488},{32,64},{40,8},{64,96},{72,40},{96,128},{104,72},{1... | collective-permute-start | bytes 786440 | tf_op jit(solution)/shard_map/ppermute | solution.py:35
  28.9 5.0 %collective-permute-start.4 = (bf16[512,256]{1,0:T(8,128)(2,1)S(1)}, bf16[512,256]{1,0:T(8,128)(2,1)S(1)}, u32[]{:S(2)}, u32[]{:S(2)}) collective-permute-start(bf16[512,256]{1,0:T(8,128)(2,1)S(1)} %collective-permute-done.2.refs_7_), channel_id=1, source_target_pairs={{0,32},{8,488},{32,64},{40,8},{64,96},{72,40},{96,128},{104,72},{1... | collective-permute-start | bytes 786440 | tf_op jit(solution)/shard_map/ppermute | solution.py:35
  37.2 5.0 %collective-permute-start.6 = (bf16[512,256]{1,0:T(8,128)(2,1)S(1)}, bf16[512,256]{1,0:T(8,128)(2,1)S(1)}, u32[]{:S(2)}, u32[]{:S(2)}) collective-permute-start(bf16[512,256]{1,0:T(8,128)(2,1)S(1)} %collective-permute-done.4.refs_9_), channel_id=1, source_target_pairs={{0,32},{8,488},{32,64},{40,8},{64,96},{72,40},{96,128},{104,72},{1... | collective-permute-start | bytes 786440 | tf_op jit(solution)/shard_map/ppermute | solution.py:35
  45.8 4.8 %collective-permute-start.8 = (bf16[512,256]{1,0:T(8,128)(2,1)S(1)}, bf16[512,256]{1,0:T(8,128)(2,1)S(1)}, u32[]{:S(2)}, u32[]{:S(2)}) collective-permute-start(bf16[512,256]{1,0:T(8,128)(2,1)S(1)} %collective-permute-done.6.refs_11_), channel_id=1, source_target_pairs={{0,32},{8,488},{32,64},{40,8},{64,96},{72,40},{96,128},{104,72},{1... | collective-permute-start | bytes 786440 | tf_op jit(solution)/shard_map/ppermute | solution.py:35
  55.7 3.1 %collective-permute-start.10 = (bf16[512,256]{1,0:T(8,128)(2,1)S(1)}, bf16[512,256]{1,0:T(8,128)(2,1)S(1)}, u32[]{:S(2)}, u32[]{:S(2)}) collective-permute-start(bf16[512,256]{1,0:T(8,128)(2,1)S(1)} %collective-permute-done.8.refs_13_), channel_id=1, source_target_pairs={{0,32},{8,488},{32,64},{40,8},{64,96},{72,40},{96,128},{104,72},{1... | collective-permute-start | bytes 786440 | tf_op jit(solution)/shard_map/ppermute | solution.py:35
  62.8 4.3 %collective-permute-start.12 = (bf16[512,256]{1,0:T(8,128)(2,1)S(1)}, bf16[512,256]{1,0:T(8,128)(2,1)S(1)}, u32[]{:S(2)}, u32[]{:S(2)}) collective-permute-start(bf16[512,256]{1,0:T(8,128)(2,1)S(1)} %collective-permute-done.10.refs_15_), channel_id=1, source_target_pairs={{0,32},{8,488},{32,64},{40,8},{64,96},{72,40},{96,128},{104,72},{1... | collective-permute-start | bytes 786440 | tf_op jit(solution)/shard_map/ppermute | solution.py:35
  67.2 2.9 %collective-permute-start.13 = (bf16[512,256]{1,0:T(8,128)(2,1)}, bf16[512,256]{1,0:T(8,128)(2,1)S(1)}, u32[]{:S(2)}, u32[]{:S(2)}) collective-permute-start(bf16[512,256]{1,0:T(8,128)(2,1)} %collective-permute-done.11.refs_16_), channel_id=1, source_target_pairs={{0,32},{8,488},{32,64},{40,8},{64,96},{72,40},{96,128},{104,72},{1... | collective-permute-start | bytes 786440 | tf_op jit(solution)/shard_map/ppermute | solution.py:35
  71.1 4.7 %collective-permute-start.16 = (bf16[2048,256]{1,0:T(8,128)(2,1)}, bf16[2048,256]{1,0:T(8,128)(2,1)}, u32[]{:S(2)}, u32[]{:S(2)}) collective-permute-start(bf16[2048,256]{1,0:T(8,128)(2,1)} %pad_maximum_fusion), channel_id=1, source_target_pairs={{0,8},{8,0},{1,9},{9,1},{2,10},{10,2},{3,11},{11,3},{4,12},{12,4},... | collective-permute-start | bytes 3145736 | tf_op jit(solution)/shard_map/ppermute | solution.py:39
  79.3 4.3 %collective-permute-start.18 = (bf16[2048,256]{1,0:T(8,128)(2,1)S(1)}, bf16[2048,256]{1,0:T(8,128)(2,1)}, u32[]{:S(2)}, u32[]{:S(2)}) collective-permute-start(bf16[2048,256]{1,0:T(8,128)(2,1)S(1)} %pad_maximum_fusion.2), channel_id=1, source_target_pairs={{0,8},{8,0},{1,9},{9,1},{2,10},{10,2},{3,11},{11,3},{4,12},{12,4},... | collective-permute-start | bytes 3145736 | tf_op jit(solution)/shard_map/ppermute | solution.py:39
  83.9 2.9 %collective-permute-start.14 = (bf16[512,256]{1,0:T(8,128)(2,1)}, bf16[512,256]{1,0:T(8,128)(2,1)S(1)}, u32[]{:S(2)}, u32[]{:S(2)}) collective-permute-start(bf16[512,256]{1,0:T(8,128)(2,1)} %copy-done.15), channel_id=1, source_target_pairs={{0,32},{8,488},{32,64},{40,8},{64,96},{72,40},{96,128},{104,72},{1... | collective-permute-start | bytes 786440 | tf_op jit(solution)/shard_map/ppermute | solution.py:35
  91.5 2.9 %collective-permute-done.15.refs_20_ = bf16[512,256]{1,0:T(8,128)(2,1)S(1)} collective-permute-done((bf16[512,256]{1,0:T(8,128)(2,1)}, bf16[512,256]{1,0:T(8,128)(2,1)S(1)}, u32[]{:S(2)}, u32[]{:S(2)}) %collective-permute-start.15) | collective-permute-done | bytes 262176 | tf_op jit(solution)/shard_map/ppermute | solution.py:35
  95.3 3.8 %collective-permute-start.19 = (bf16[1024,256]{1,0:T(8,128)(2,1)}, bf16[1024,256]{1,0:T(8,128)(2,1)}, u32[]{:S(2)}, u32[]{:S(2)}) collective-permute-start(bf16[1024,256]{1,0:T(8,128)(2,1)} %pad_maximum_fusion.3), channel_id=1, source_target_pairs={{0,8},{8,0},{1,9},{9,1},{2,10},{10,2},{3,11},{11,3},{4,12},{12,4},... | collective-permute-start | bytes 1572872 | tf_op jit(solution)/shard_map/ppermute | solution.py:39
  106.6 2.9 %collective-permute-done.21.refs_26_ = bf16[512,256]{1,0:T(8,128)(2,1)} collective-permute-done((bf16[512,256]{1,0:T(8,128)(2,1)S(1)}, bf16[512,256]{1,0:T(8,128)(2,1)}, u32[]{:S(2)}, u32[]{:S(2)}) %collective-permute-start.21) | collective-permute-done | bytes 262176 | tf_op jit(solution)/shard_map/ppermute | solution.py:35
  109.6 10.7 %forward.1 = (f32[2,128,512]{2,1,0:T(8,128)S(1)}, f32[2,2688,512]{2,1,0:T(8,128)S(1)}, bf16[5504,256]{1,0:T(8,128)(2,1)S(1)}, f32[8,4,128]{2,1,0:T(4,128)S(1)}) custom-call(s32[2,21]{1,0:T(2,128)S(1)} %compare_select_fusion.7.refs_0_, s32[128]{0:T(128)S(1)} %get-tuple-element.77.refs_1_, bf16[256,512]{1,0:T(8,128)(2,1)S(1)} %copy-done, ...), custom_call_target="tpu_custom_call" | custom-call | flops 1409286144 | bytes 16777216 | tf_op jit(solution)/shard_map/forward/pallas_call | solution.py:352
  120.3 10.0 %all_to_all.5.refs_2_.refs_1_ = f32[8,4,128]{2,1,0:T(4,128)S(1)} all-to-all(f32[8,4,128]{2,1,0:T(4,128)S(1)} %get-tuple-element.40), channel_id=1, replica_groups=mesh['z'=16,'xh'=2,'core'=2,'y'=4,'xl'=2] {'y','xl'}, dimensions={0} | all-to-all | bytes 32768 | tf_op jit(solution)/shard_map/all_to_all | solution.py:90
  130.2 9.6 %backward.1 = (bf16[2,2688,512]{2,1,0:T(8,128)(2,1)S(1)}, bf16[8192,256]{1,0:T(8,128)(2,1)S(1)}, bf16[3072,256]{1,0:T(8,128)(2,1)S(1)}, bf16[2048,256]{1,0:T(8,1...) custom-call(s32[2,21]{1,0:T(2,128)S(1)} %compare_select_fusion.7.refs_0_, ...), custom_call_target="tpu_custom_call" | custom-call | flops 2113929216 | bytes 33554432 | tf_op jit(solution)/shard_map/backward/pallas_call | solution.py:373
  139.9 4.9 %collective-permute-start.24 = (bf16[2048,256]{1,0:T(8,128)(2,1)S(1)}, bf16[2048,256]{1,0:T(8,128)(2,1)S(1)}, u32[]{:S(2)}, u32[]{:S(2)}) collective-permute-start(bf16[2048,256]{1,0:T(8,128)(2,1)S(1)} %get-tuple-element.50), channel_id=1, source_target_pairs={{0,8},{8,0},{1,9},{9,1},{2,10},{10,2},{3,11},{11,3},{4,12},{12,4},... | collective-permute-start | bytes 3145736 | tf_op jit(solution)/shard_map/ppermute | solution.py:39
  144.8 2.8 %collective-permute-start.23 = (bf16[512,256]{1,0:T(8,128)(2,1)S(1)}, bf16[512,256]{1,0:T(8,128)(2,1)S(1)}, u32[]{:S(2)}, u32[]{:S(2)}) collective-permute-start(bf16[512,256]{1,0:T(8,128)(2,1)S(1)} %get-tuple-element.48), channel_id=1, source_target_pairs={{0,32},{8,488},{32,64},{40,8},{64,96},{72,40},{96,128},{104,72},{1... | collective-permute-start | bytes 786440 | tf_op jit(solution)/shard_map/ppermute | solution.py:35
  149.6 3.9 %collective-permute-start.22 = (bf16[512,256]{1,0:T(8,128)(2,1)S(1)}, bf16[512,256]{1,0:T(8,128)(2,1)S(1)}, u32[]{:S(2)}, u32[]{:S(2)}) collective-permute-start(bf16[512,256]{1,0:T(8,128)(2,1)S(1)} %get-tuple-element.47), channel_id=1, source_target_pairs={{0,32},{8,488},{32,64},{40,8},{64,96},{72,40},{96,128},{104,72},{1... | collective-permute-start | bytes 786440 | tf_op jit(solution)/shard_map/ppermute | solution.py:35
  158.4 4.9 %collective-permute-start.25 = (bf16[512,256]{1,0:T(8,128)(2,1)S(1)}, bf16[512,256]{1,0:T(8,128)(2,1)S(1)}, u32[]{:S(2)}, u32[]{:S(2)}) collective-permute-start(bf16[512,256]{1,0:T(8,128)(2,1)S(1)} %add_convert_fusion.13), channel_id=1, source_target_pairs={{0,32},{8,488},{32,64},{40,8},{64,96},{72,40},{96,128},{104,72},{1... | collective-permute-start | bytes 786440 | tf_op jit(solution)/shard_map/ppermute | solution.py:35
  166.6 5.0 %collective-permute-start.27 = (bf16[512,256]{1,0:T(8,128)(2,1)S(1)}, bf16[512,256]{1,0:T(8,128)(2,1)S(1)}, u32[]{:S(2)}, u32[]{:S(2)}) collective-permute-start(bf16[512,256]{1,0:T(8,128)(2,1)S(1)} %add_convert_fusion.11), channel_id=1, source_target_pairs={{0,32},{8,488},{32,64},{40,8},{64,96},{72,40},{96,128},{104,72},{1... | collective-permute-start | bytes 786440 | tf_op jit(solution)/shard_map/ppermute | solution.py:35
  175.1 5.0 %collective-permute-start.30 = (bf16[512,256]{1,0:T(8,128)(2,1)S(1)}, bf16[512,256]{1,0:T(8,128)(2,1)S(1)}, u32[]{:S(2)}, u32[]{:S(2)}) collective-permute-start(bf16[512,256]{1,0:T(8,128)(2,1)S(1)} %add_convert_fusion.9), channel_id=1, source_target_pairs={{0,32},{8,488},{32,64},{40,8},{64,96},{72,40},{96,128},{104,72},{1... | collective-permute-start | bytes 786440 | tf_op jit(solution)/shard_map/ppermute | solution.py:35
  183.5 5.0 %collective-permute-start.32 = (bf16[512,256]{1,0:T(8,128)(2,1)S(1)}, bf16[512,256]{1,0:T(8,128)(2,1)S(1)}, u32[]{:S(2)}, u32[]{:S(2)}) collective-permute-start(bf16[512,256]{1,0:T(8,128)(2,1)S(1)} %add_convert_fusion.7), channel_id=1, source_target_pairs={{0,32},{8,488},{32,64},{40,8},{64,96},{72,40},{96,128},{104,72},{1... | collective-permute-start | bytes 786440 | tf_op jit(solution)/shard_map/ppermute | solution.py:35
  192.0 5.0 %collective-permute-start.35 = (bf16[512,256]{1,0:T(8,128)(2,1)S(1)}, bf16[512,256]{1,0:T(8,128)(2,1)S(1)}, u32[]{:S(2)}, u32[]{:S(2)}) collective-permute-start(bf16[512,256]{1,0:T(8,128)(2,1)S(1)} %add_convert_fusion.5), channel_id=1, source_target_pairs={{0,32},{8,488},{32,64},{40,8},{64,96},{72,40},{96,128},{104,72},{1... | collective-permute-start | bytes 786440 | tf_op jit(solution)/shard_map/ppermute | solution.py:35
  200.4 5.0 %collective-permute-start.37 = (bf16[512,256]{1,0:T(8,128)(2,1)S(1)}, bf16[512,256]{1,0:T(8,128)(2,1)S(1)}, u32[]{:S(2)}, u32[]{:S(2)}) collective-permute-start(bf16[512,256]{1,0:T(8,128)(2,1)S(1)} %add_convert_fusion.3), channel_id=1, source_target_pairs={{0,32},{8,488},{32,64},{40,8},{64,96},{72,40},{96,128},{104,72},{1... | collective-permute-start | bytes 786440 | tf_op jit(solution)/shard_map/ppermute | solution.py:35
  208.8 5.0 %collective-permute-start.39 = (bf16[512,256]{1,0:T(8,128)(2,1)S(1)}, bf16[512,256]{1,0:T(8,128)(2,1)S(1)}, u32[]{:S(2)}, u32[]{:S(2)}) collective-permute-start(bf16[512,256]{1,0:T(8,128)(2,1)S(1)} %add_convert_fusion.1), channel_id=1, source_target_pairs={{0,32},{8,488},{32,64},{40,8},{64,96},{72,40},{96,128},{104,72},{1... | collective-permute-start | bytes 786440 | tf_op jit(solution)/shard_map/ppermute | solution.py:35
  213.9 3.2 %collective-permute-done.39 = bf16[512,256]{1,0:T(8,128)(2,1)S(1)} collective-permute-done((bf16[512,256]{1,0:T(8,128)(2,1)S(1)}, bf16[512,256]{1,0:T(8,128)(2,1)S(1)}, u32[]{:S(2)}, u32[]{:S(2)}) %collective-permute-start.39) | collective-permute-done | bytes 262176 | tf_op jit(solution)/shard_map/ppermute | solution.py:35
  217.2 4.5 %collective-permute-start.43 = (bf16[256,256]{1,0:T(8,128)(2,1)S(1)}, bf16[256,256]{1,0:T(8,128)(2,1)S(1)}, u32[]{:S(2)}, u32[]{:S(2)}) collective-permute-start(bf16[256,256]{1,0:T(8,128)(2,1)S(1)} %slice.194), channel_id=1, source_target_pairs={{0,16},{16,0},{1,17},{17,1},{2,18},{18,2},{3,19},{19,3},{4,20},{20... | collective-permute-start | bytes 393224 | tf_op jit(solution)/shard_map/ppermute | solution.py:85
  221.7 11.8 %collective-permute-start.41 = (bf16[256,256]{1,0:T(8,128)(2,1)S(1)}, bf16[256,256]{1,0:T(8,128)(2,1)S(1)}, u32[]{:S(2)}, u32[]{:S(2)}) collective-permute-start(bf16[256,256]{1,0:T(8,128)(2,1)S(1)} %get-tuple-element.82), channel_id=1, source_target_pairs={{0,8},{8,0},{1,9},{9,1},{2,10},{10,2},{3,11},{11,3},{4,12},{12,4},... | collective-permute-start | bytes 393224 | tf_op jit(solution)/shard_map/ppermute | solution.py:39
  238.0 4.0 %collective-permute-done.42 = bf16[256,256]{1,0:T(8,128)(2,1)S(1)} collective-permute-done((bf16[256,256]{1,0:T(8,128)(2,1)S(1)}, bf16[256,256]{1,0:T(8,128)(2,1)S(1)}, u32[]{:S(2)}, u32[]{:S(2)}) %collective-permute-start.42) | collective-permute-done | bytes 131104 | tf_op jit(solution)/shard_map/ppermute | solution.py:82
  (142 shorter events, 73.2 us)
Async XLA Ops:
  10.2 15.4 %collective-permute-start.1 = (bf16[512,256]{1,0:T(8,128)(2,1)S(1)}, bf16[512,256]{1,0:T(8,128)(2,1)S(1)}, u32[]{:S(2)}, u32[]{:S(2)}) collective-permute-start(bf16[512,256]{1,0:T(8,128)(2,1)S(1)} %pad_maximum_fusion.4.refs_5_), channel_id=1, source_target_pairs={{0,8},{8,0},{1,9},{9,1},{2,10},{10,2},{3,11},{11,3},{4,12},{12,4},... | collective-permute-start | bytes 786440 | tf_op jit(solution)/shard_map/ppermute | solution.py:39
  19.5 9.3 %collective-permute-start.2 = (bf16[512,256]{1,0:T(8,128)(2,1)S(1)}, bf16[512,256]{1,0:T(8,128)(2,1)S(1)}, u32[]{:S(2)}, u32[]{:S(2)}) collective-permute-start(bf16[512,256]{1,0:T(8,128)(2,1)S(1)} %pad_maximum_fusion.4.refs_5_), channel_id=1, source_target_pairs={{0,32},{8,488},{32,64},{40,8},{64,96},{72,40},{96,128},{104,72},{1... | collective-permute-start | bytes 786440 | tf_op jit(solution)/shard_map/ppermute | solution.py:35
  25.6 8.3 %collective-permute-start.3 = (bf16[512,256]{1,0:T(8,128)(2,1)S(1)}, bf16[512,256]{1,0:T(8,128)(2,1)S(1)}, u32[]{:S(2)}, u32[]{:S(2)}) collective-permute-start(bf16[512,256]{1,0:T(8,128)(2,1)S(1)} %collective-permute-done.1.refs_6_), channel_id=1, source_target_pairs={{0,32},{8,488},{32,64},{40,8},{64,96},{72,40},{96,128},{104,72},{1... | collective-permute-start | bytes 786440 | tf_op jit(solution)/shard_map/ppermute | solution.py:35
  28.9 8.3 %collective-permute-start.4 = (bf16[512,256]{1,0:T(8,128)(2,1)S(1)}, bf16[512,256]{1,0:T(8,128)(2,1)S(1)}, u32[]{:S(2)}, u32[]{:S(2)}) collective-permute-start(bf16[512,256]{1,0:T(8,128)(2,1)S(1)} %collective-permute-done.2.refs_7_), channel_id=1, source_target_pairs={{0,32},{8,488},{32,64},{40,8},{64,96},{72,40},{96,128},{104,72},{1... | collective-permute-start | bytes 786440 | tf_op jit(solution)/shard_map/ppermute | solution.py:35
  37.2 8.6 %collective-permute-start.6 = (bf16[512,256]{1,0:T(8,128)(2,1)S(1)}, bf16[512,256]{1,0:T(8,128)(2,1)S(1)}, u32[]{:S(2)}, u32[]{:S(2)}) collective-permute-start(bf16[512,256]{1,0:T(8,128)(2,1)S(1)} %collective-permute-done.4.refs_9_), channel_id=1, source_target_pairs={{0,32},{8,488},{32,64},{40,8},{64,96},{72,40},{96,128},{104,72},{1... | collective-permute-start | bytes 786440 | tf_op jit(solution)/shard_map/ppermute | solution.py:35
  45.8 9.9 %collective-permute-start.8 = (bf16[512,256]{1,0:T(8,128)(2,1)S(1)}, bf16[512,256]{1,0:T(8,128)(2,1)S(1)}, u32[]{:S(2)}, u32[]{:S(2)}) collective-permute-start(bf16[512,256]{1,0:T(8,128)(2,1)S(1)} %collective-permute-done.6.refs_11_), channel_id=1, source_target_pairs={{0,32},{8,488},{32,64},{40,8},{64,96},{72,40},{96,128},{104,72},{1... | collective-permute-start | bytes 786440 | tf_op jit(solution)/shard_map/ppermute | solution.py:35
  62.8 15.3 %collective-permute-start.12 = (bf16[512,256]{1,0:T(8,128)(2,1)S(1)}, bf16[512,256]{1,0:T(8,128)(2,1)S(1)}, u32[]{:S(2)}, u32[]{:S(2)}) collective-permute-start(bf16[512,256]{1,0:T(8,128)(2,1)S(1)} %collective-permute-done.10.refs_15_), channel_id=1, source_target_pairs={{0,32},{8,488},{32,64},{40,8},{64,96},{72,40},{96,128},{104,72},{1... | collective-permute-start | bytes 786440 | tf_op jit(solution)/shard_map/ppermute | solution.py:35
  67.2 11.0 %collective-permute-start.13 = (bf16[512,256]{1,0:T(8,128)(2,1)}, bf16[512,256]{1,0:T(8,128)(2,1)S(1)}, u32[]{:S(2)}, u32[]{:S(2)}) collective-permute-start(bf16[512,256]{1,0:T(8,128)(2,1)} %collective-permute-done.11.refs_16_), channel_id=1, source_target_pairs={{0,32},{8,488},{32,64},{40,8},{64,96},{72,40},{96,128},{104,72},{1... | collective-permute-start | bytes 786440 | tf_op jit(solution)/shard_map/ppermute | solution.py:35
  71.1 30.9 %collective-permute-start.16 = (bf16[2048,256]{1,0:T(8,128)(2,1)}, bf16[2048,256]{1,0:T(8,128)(2,1)}, u32[]{:S(2)}, u32[]{:S(2)}) collective-permute-start(bf16[2048,256]{1,0:T(8,128)(2,1)} %pad_maximum_fusion), channel_id=1, source_target_pairs={{0,8},{8,0},{1,9},{9,1},{2,10},{10,2},{3,11},{11,3},{4,12},{12,4},... | collective-permute-start | bytes 3145736 | tf_op jit(solution)/shard_map/ppermute | solution.py:39
  76.0 33.5 %collective-permute-start.17 = (bf16[2048,256]{1,0:T(8,128)(2,1)S(1)}, bf16[2048,256]{1,0:T(8,128)(2,1)}, u32[]{:S(2)}, u32[]{:S(2)}) collective-permute-start(bf16[2048,256]{1,0:T(8,128)(2,1)S(1)} %pad_maximum_fusion.1), channel_id=1, source_target_pairs={{0,8},{8,0},{1,9},{9,1},{2,10},{10,2},{3,11},{11,3},{4,12},{12,4},... | collective-permute-start | bytes 3145736 | tf_op jit(solution)/shard_map/ppermute | solution.py:39
  79.3 30.2 %collective-permute-start.18 = (bf16[2048,256]{1,0:T(8,128)(2,1)S(1)}, bf16[2048,256]{1,0:T(8,128)(2,1)}, u32[]{:S(2)}, u32[]{:S(2)}) collective-permute-start(bf16[2048,256]{1,0:T(8,128)(2,1)S(1)} %pad_maximum_fusion.2), channel_id=1, source_target_pairs={{0,8},{8,0},{1,9},{9,1},{2,10},{10,2},{3,11},{11,3},{4,12},{12,4},... | collective-permute-start | bytes 3145736 | tf_op jit(solution)/shard_map/ppermute | solution.py:39
  95.3 14.2 %collective-permute-start.19 = (bf16[1024,256]{1,0:T(8,128)(2,1)}, bf16[1024,256]{1,0:T(8,128)(2,1)}, u32[]{:S(2)}, u32[]{:S(2)}) collective-permute-start(bf16[1024,256]{1,0:T(8,128)(2,1)} %pad_maximum_fusion.3), channel_id=1, source_target_pairs={{0,8},{8,0},{1,9},{9,1},{2,10},{10,2},{3,11},{11,3},{4,12},{12,4},... | collective-permute-start | bytes 1572872 | tf_op jit(solution)/shard_map/ppermute | solution.py:39
  139.9 13.7 %collective-permute-start.24 = (bf16[2048,256]{1,0:T(8,128)(2,1)S(1)}, bf16[2048,256]{1,0:T(8,128)(2,1)S(1)}, u32[]{:S(2)}, u32[]{:S(2)}) collective-permute-start(bf16[2048,256]{1,0:T(8,128)(2,1)S(1)} %get-tuple-element.50), channel_id=1, source_target_pairs={{0,8},{8,0},{1,9},{9,1},{2,10},{10,2},{3,11},{11,3},{4,12},{12,4},... | collective-permute-start | bytes 3145736 | tf_op jit(solution)/shard_map/ppermute | solution.py:39
  144.8 8.7 %collective-permute-start.23 = (bf16[512,256]{1,0:T(8,128)(2,1)S(1)}, bf16[512,256]{1,0:T(8,128)(2,1)S(1)}, u32[]{:S(2)}, u32[]{:S(2)}) collective-permute-start(bf16[512,256]{1,0:T(8,128)(2,1)S(1)} %get-tuple-element.48), channel_id=1, source_target_pairs={{0,32},{8,488},{32,64},{40,8},{64,96},{72,40},{96,128},{104,72},{1... | collective-permute-start | bytes 786440 | tf_op jit(solution)/shard_map/ppermute | solution.py:35
  147.7 24.0 %collective-permute-start.29 = (bf16[2048,256]{1,0:T(8,128)(2,1)S(1)}, bf16[2048,256]{1,0:T(8,128)(2,1)S(1)}, u32[]{:S(2)}, u32[]{:S(2)}) collective-permute-start(bf16[2048,256]{1,0:T(8,128)(2,1)S(1)} %get-tuple-element.57), channel_id=1, source_target_pairs={{0,8},{8,0},{1,9},{9,1},{2,10},{10,2},{3,11},{11,3},{4,12},{12,4},... | collective-permute-start | bytes 3145736 | tf_op jit(solution)/shard_map/ppermute | solution.py:39
  149.6 8.7 %collective-permute-start.22 = (bf16[512,256]{1,0:T(8,128)(2,1)S(1)}, bf16[512,256]{1,0:T(8,128)(2,1)S(1)}, u32[]{:S(2)}, u32[]{:S(2)}) collective-permute-start(bf16[512,256]{1,0:T(8,128)(2,1)S(1)} %get-tuple-element.47), channel_id=1, source_target_pairs={{0,32},{8,488},{32,64},{40,8},{64,96},{72,40},{96,128},{104,72},{1... | collective-permute-start | bytes 786440 | tf_op jit(solution)/shard_map/ppermute | solution.py:35
  153.7 9.6 %collective-permute-start.26 = (bf16[512,256]{1,0:T(8,128)(2,1)S(1)}, bf16[512,256]{1,0:T(8,128)(2,1)S(1)}, u32[]{:S(2)}, u32[]{:S(2)}) collective-permute-start(bf16[512,256]{1,0:T(8,128)(2,1)S(1)} %add_convert_fusion.14), channel_id=1, source_target_pairs={{0,32},{8,488},{32,64},{40,8},{64,96},{72,40},{96,128},{104,72},{1... | collective-permute-start | bytes 786440 | tf_op jit(solution)/shard_map/ppermute | solution.py:35
  156.1 32.5 %collective-permute-start.34 = (bf16[3072,256]{1,0:T(8,128)(2,1)S(1)}, bf16[3072,256]{1,0:T(8,128)(2,1)S(1)}, u32[]{:S(2)}, u32[]{:S(2)}) collective-permute-start(bf16[3072,256]{1,0:T(8,128)(2,1)S(1)} %get-tuple-element.64), channel_id=1, source_target_pairs={{0,8},{8,0},{1,9},{9,1},{2,10},{10,2},{3,11},{11,3},{4,12},{12,4},... | collective-permute-start | bytes 4718600 | tf_op jit(solution)/shard_map/ppermute | solution.py:39
  163.4 8.3 %collective-permute-start.28 = (bf16[512,256]{1,0:T(8,128)(2,1)S(1)}, bf16[512,256]{1,0:T(8,128)(2,1)S(1)}, u32[]{:S(2)}, u32[]{:S(2)}) collective-permute-start(bf16[512,256]{1,0:T(8,128)(2,1)S(1)} %add_convert_fusion.12), channel_id=1, source_target_pairs={{0,32},{8,488},{32,64},{40,8},{64,96},{72,40},{96,128},{104,72},{1... | collective-permute-start | bytes 786440 | tf_op jit(solution)/shard_map/ppermute | solution.py:35
  166.6 8.3 %collective-permute-start.27 = (bf16[512,256]{1,0:T(8,128)(2,1)S(1)}, bf16[512,256]{1,0:T(8,128)(2,1)S(1)}, u32[]{:S(2)}, u32[]{:S(2)}) collective-permute-start(bf16[512,256]{1,0:T(8,128)(2,1)S(1)} %add_convert_fusion.11), channel_id=1, source_target_pairs={{0,32},{8,488},{32,64},{40,8},{64,96},{72,40},{96,128},{104,72},{1... | collective-permute-start | bytes 786440 | tf_op jit(solution)/shard_map/ppermute | solution.py:35
  171.8 8.3 %collective-permute-start.31 = (bf16[512,256]{1,0:T(8,128)(2,1)S(1)}, bf16[512,256]{1,0:T(8,128)(2,1)S(1)}, u32[]{:S(2)}, u32[]{:S(2)}) collective-permute-start(bf16[512,256]{1,0:T(8,128)(2,1)S(1)} %add_convert_fusion.10), channel_id=1, source_target_pairs={{0,32},{8,488},{32,64},{40,8},{64,96},{72,40},{96,128},{104,72},{1... | collective-permute-start | bytes 786440 | tf_op jit(solution)/shard_map/ppermute | solution.py:35
  175.1 8.3 %collective-permute-start.30 = (bf16[512,256]{1,0:T(8,128)(2,1)S(1)}, bf16[512,256]{1,0:T(8,128)(2,1)S(1)}, u32[]{:S(2)}, u32[]{:S(2)}) collective-permute-start(bf16[512,256]{1,0:T(8,128)(2,1)S(1)} %add_convert_fusion.9), channel_id=1, source_target_pairs={{0,32},{8,488},{32,64},{40,8},{64,96},{72,40},{96,128},{104,72},{1... | collective-permute-start | bytes 786440 | tf_op jit(solution)/shard_map/ppermute | solution.py:35
  180.2 8.3 %collective-permute-start.33 = (bf16[512,256]{1,0:T(8,128)(2,1)S(1)}, bf16[512,256]{1,0:T(8,128)(2,1)S(1)}, u32[]{:S(2)}, u32[]{:S(2)}) collective-permute-start(bf16[512,256]{1,0:T(8,128)(2,1)S(1)} %add_convert_fusion.8), channel_id=1, source_target_pairs={{0,32},{8,488},{32,64},{40,8},{64,96},{72,40},{96,128},{104,72},{1... | collective-permute-start | bytes 786440 | tf_op jit(solution)/shard_map/ppermute | solution.py:35
  183.5 8.3 %collective-permute-start.32 = (bf16[512,256]{1,0:T(8,128)(2,1)S(1)}, bf16[512,256]{1,0:T(8,128)(2,1)S(1)}, u32[]{:S(2)}, u32[]{:S(2)}) collective-permute-start(bf16[512,256]{1,0:T(8,128)(2,1)S(1)} %add_convert_fusion.7), channel_id=1, source_target_pairs={{0,32},{8,488},{32,64},{40,8},{64,96},{72,40},{96,128},{104,72},{1... | collective-permute-start | bytes 786440 | tf_op jit(solution)/shard_map/ppermute | solution.py:35
  192.0 8.3 %collective-permute-start.35 = (bf16[512,256]{1,0:T(8,128)(2,1)S(1)}, bf16[512,256]{1,0:T(8,128)(2,1)S(1)}, u32[]{:S(2)}, u32[]{:S(2)}) collective-permute-start(bf16[512,256]{1,0:T(8,128)(2,1)S(1)} %add_convert_fusion.5), channel_id=1, source_target_pairs={{0,32},{8,488},{32,64},{40,8},{64,96},{72,40},{96,128},{104,72},{1... | collective-permute-start | bytes 786440 | tf_op jit(solution)/shard_map/ppermute | solution.py:35
  197.1 8.3 %collective-permute-start.38 = (bf16[512,256]{1,0:T(8,128)(2,1)S(1)}, bf16[512,256]{1,0:T(8,128)(2,1)S(1)}, u32[]{:S(2)}, u32[]{:S(2)}) collective-permute-start(bf16[512,256]{1,0:T(8,128)(2,1)S(1)} %add_convert_fusion.4), channel_id=1, source_target_pairs={{0,32},{8,488},{32,64},{40,8},{64,96},{72,40},{96,128},{104,72},{1... | collective-permute-start | bytes 786440 | tf_op jit(solution)/shard_map/ppermute | solution.py:35
  200.4 8.3 %collective-permute-start.37 = (bf16[512,256]{1,0:T(8,128)(2,1)S(1)}, bf16[512,256]{1,0:T(8,128)(2,1)S(1)}, u32[]{:S(2)}, u32[]{:S(2)}) collective-permute-start(bf16[512,256]{1,0:T(8,128)(2,1)S(1)} %add_convert_fusion.3), channel_id=1, source_target_pairs={{0,32},{8,488},{32,64},{40,8},{64,96},{72,40},{96,128},{104,72},{1... | collective-permute-start | bytes 786440 | tf_op jit(solution)/shard_map/ppermute | solution.py:35
  205.5 8.3 %collective-permute-start.40 = (bf16[512,256]{1,0:T(8,128)(2,1)S(1)}, bf16[512,256]{1,0:T(8,128)(2,1)S(1)}, u32[]{:S(2)}, u32[]{:S(2)}) collective-permute-start(bf16[512,256]{1,0:T(8,128)(2,1)S(1)} %add_convert_fusion.2), channel_id=1, source_target_pairs={{0,32},{8,488},{32,64},{40,8},{64,96},{72,40},{96,128},{104,72},{1... | collective-permute-start | bytes 786440 | tf_op jit(solution)/shard_map/ppermute | solution.py:35
  208.8 8.3 %collective-permute-start.39 = (bf16[512,256]{1,0:T(8,128)(2,1)S(1)}, bf16[512,256]{1,0:T(8,128)(2,1)S(1)}, u32[]{:S(2)}, u32[]{:S(2)}) collective-permute-start(bf16[512,256]{1,0:T(8,128)(2,1)S(1)} %add_convert_fusion.1), channel_id=1, source_target_pairs={{0,32},{8,488},{32,64},{40,8},{64,96},{72,40},{96,128},{104,72},{1... | collective-permute-start | bytes 786440 | tf_op jit(solution)/shard_map/ppermute | solution.py:35
  217.2 20.8 %collective-permute-start.43 = (bf16[256,256]{1,0:T(8,128)(2,1)S(1)}, bf16[256,256]{1,0:T(8,128)(2,1)S(1)}, u32[]{:S(2)}, u32[]{:S(2)}) collective-permute-start(bf16[256,256]{1,0:T(8,128)(2,1)S(1)} %slice.194), channel_id=1, source_target_pairs={{0,16},{16,0},{1,17},{17,1},{2,18},{18,2},{3,19},{19,3},{4,20},{20... | collective-permute-start | bytes 393224 | tf_op jit(solution)/shard_map/ppermute | solution.py:85
  221.7 16.3 %collective-permute-start.41 = (bf16[256,256]{1,0:T(8,128)(2,1)S(1)}, bf16[256,256]{1,0:T(8,128)(2,1)S(1)}, u32[]{:S(2)}, u32[]{:S(2)}) collective-permute-start(bf16[256,256]{1,0:T(8,128)(2,1)S(1)} %get-tuple-element.82), channel_id=1, source_target_pairs={{0,8},{8,0},{1,9},{9,1},{2,10},{10,2},{3,11},{11,3},{4,12},{12,4},... | collective-permute-start | bytes 393224 | tf_op jit(solution)/shard_map/ppermute | solution.py:39
  233.5 8.5 %collective-permute-start.42 = (bf16[256,256]{1,0:T(8,128)(2,1)S(1)}, bf16[256,256]{1,0:T(8,128)(2,1)S(1)}, u32[]{:S(2)}, u32[]{:S(2)}) collective-permute-start(bf16[256,256]{1,0:T(8,128)(2,1)S(1)} %get-tuple-element.83), channel_id=1, source_target_pairs={{0,24},{8,16},{16,8},{24,0},{1,25},{9,17},{17,9},{25,1},{2,26},{10... | collective-permute-start | bytes 393224 | tf_op jit(solution)/shard_map/ppermute | solution.py:82
  (31 other events, 582.0 us)

commit v2 on v1

--- a/solution.py
+++ b/solution.py
@@ -18,8 +18,8 @@
 SWAP = [(0, 1), (1, 0)]
 NBLK = 128
 PART = 4 * BLOCK
-SWAP_AFTER = (2, 4, 6, 7)
-GATHERED = [1] * 16 + [4, 4, 4, 2, 1, 1]
+SWAP_AFTER = (2, 5, 7)
+GATHERED = [1] * 16 + [4, 6, 4, 1, 1]
 SENT = [16, 6, 4, 4, 1, 1]
 F32 = jnp.float32
 BF16 = jnp.bfloat16
@@ -79,11 +79,10 @@
     rows = PART // 2
     other = total(ring(other), part_of(mine, 1)).astype(BF16)
     other, mine = lax.optimization_barrier((other, mine))
-    across = lax.ppermute(other[rows:], ("xh", "core"), [(i, 3 - i) for i in range(4)])
-    near_core = swap(other[:rows])
-    own = total(ring(own), part_of(mine, 0))
+    own = ring(own)
+    own = total(own, part_of(mine, 0), swap(other))
     mate = lax.ppermute(own[rows:].astype(BF16), "xh", SWAP)
-    return total(own[:rows], near_core, across, mate)
+    return total(own[:rows], mate)
 
 
 def head_copies(x):
@@ -205,7 +204,7 @@
 
     def weigh(keys, query):
         score = dot(keys, query)
-        return 1.0 / (1.0 + jnp.exp(shift - score * scale))
+        return 1.0 / (1.0 + jnp.exp2(shift * math.log2(math.e) - score * (scale * math.log2(math.e))))
 
     for q in range(per_device):
         own = await_slot(q, 0)

time: 244 us -> 231 us (0.947)
  the two profiles are of different devices: /device:TPU:1 before, /device:TPU:4 now
where the time goes in v2:
time: 231 us; the launch traced here: 230 us
  starting transfers between devices  104 us (45%)
  waiting for transfers between devices  75.6 us (33%)
  Pallas kernels  22.1 us (10%)
  blocking collectives  11.1 us (5%)
  local copies, waits for them, and re-layouts  9.15 us (4%)
  other arithmetic  6.73 us (3%)
    ppermute x32, starting transfers between devices, ring(): return lax.ppermute(x, RING, ring_pairs())  76.9 us
    ppermute x32, waiting for transfers between devices, ring(): return lax.ppermute(x, RING, ring_pairs())  69.4 us
    ppermute x8, starting transfers between devices, swap(): return lax.ppermute(x, 'core', SWAP)  16.1 us
    all_to_all x1, blocking collectives, head_copies(): return lax.all_to_all(x, HEAD, 0, 0, tiled=True)  11.1 us
    pallas_call x1, Pallas kernels, forward(): pl.pallas_call(lambda *refs: forward_kernel(pairs, 1.0 / math.sqrt(DH), m...  10.2 us
    pallas_call x1, Pallas kernels, backward(): pl.pallas_call(lambda *refs: backward_kernel(pairs, 1.0 / math.sqrt(DH),...  9.64 us
    ppermute x1, starting transfers between devices, gather_blocks(): pair = jnp.concatenate([kv, lax.ppermute(kv, 'xh', SWAP)], axis=0)  7.76 us
    unnamed x52, local copies, waits for them, and re-layouts  5.73 us
  transfers between devices with their start and end apart: 42, of which 31 were waited for; matrix products, arithmetic and copies ran while one was open for 5% of the time, Pallas kernels for 1%

profile of v2, /device:TPU:4, one launch (start us, length us, event | category | flops | bytes accessed | tf_op | source)
XLA Modules:
  0.0 229.6 jit_solution(13546880641033792156)
XLA Ops:
  2.3 7.8 %collective-permute-start = (bf16[256,256]{1,0:T(8,128)(2,1)S(1)}, bf16[256,256]{1,0:T(8,128)(2,1)S(1)}, u32[]{:S(2)}, u32[]{:S(2)}) collective-permute-start(bf16[256,256]{1,0:T(8,128)(2,1)S(1)} %constant_dynamic-update-slice_fusion), channel_id=1, source_target_pairs={{0,16},{16,0},{1,17},{17,1},{2,18},{18,2},{3,19},{19,3},{4,20},{20... | collective-permute-start | bytes 393224 | tf_op jit(solution)/shard_map/ppermute | solution.py:43
  10.1 2.9 %collective-permute-done = bf16[256,256]{1,0:T(8,128)(2,1)S(1)} collective-permute-done((bf16[256,256]{1,0:T(8,128)(2,1)S(1)}, bf16[256,256]{1,0:T(8,128)(2,1)S(1)}, u32[]{:S(2)}, u32[]{:S(2)}) %collective-permute-start) | collective-permute-done | bytes 131104 | tf_op jit(solution)/shard_map/ppermute | solution.py:43
  17.0 3.7 %collective-permute-start.3 = (bf16[512,256]{1,0:T(8,128)(2,1)S(1)}, bf16[512,256]{1,0:T(8,128)(2,1)S(1)}, u32[]{:S(2)}, u32[]{:S(2)}) collective-permute-start(bf16[512,256]{1,0:T(8,128)(2,1)S(1)} %collective-permute-done.1.refs_6_), channel_id=1, source_target_pairs={{0,32},{8,488},{32,64},{40,8},{64,96},{72,40},{96,128},{104,72},{1... | collective-permute-start | bytes 786440 | tf_op jit(solution)/shard_map/ppermute | solution.py:35
  20.6 8.1 %collective-permute-done.2.refs_7_ = bf16[512,256]{1,0:T(8,128)(2,1)S(1)} collective-permute-done((bf16[512,256]{1,0:T(8,128)(2,1)S(1)}, bf16[512,256]{1,0:T(8,128)(2,1)S(1)}, u32[]{:S(2)}, u32[]{:S(2)}) %collective-permute-start.2) | collective-permute-done | bytes 262176 | tf_op jit(solution)/shard_map/ppermute | solution.py:35
  33.4 4.7 %collective-permute-done.4.refs_9_ = bf16[512,256]{1,0:T(8,128)(2,1)S(1)} collective-permute-done((bf16[512,256]{1,0:T(8,128)(2,1)S(1)}, bf16[512,256]{1,0:T(8,128)(2,1)S(1)}, u32[]{:S(2)}, u32[]{:S(2)}) %collective-permute-start.4) | collective-permute-done | bytes 262176 | tf_op jit(solution)/shard_map/ppermute | solution.py:35
  43.6 4.0 %collective-permute-done.6.refs_11_ = bf16[512,256]{1,0:T(8,128)(2,1)S(1)} collective-permute-done((bf16[512,256]{1,0:T(8,128)(2,1)S(1)}, bf16[512,256]{1,0:T(8,128)(2,1)S(1)}, u32[]{:S(2)}, u32[]{:S(2)}) %collective-permute-start.6) | collective-permute-done | bytes 262176 | tf_op jit(solution)/shard_map/ppermute | solution.py:35
  53.6 3.5 %collective-permute-done.8.refs_13_ = bf16[512,256]{1,0:T(8,128)(2,1)S(1)} collective-permute-done((bf16[512,256]{1,0:T(8,128)(2,1)S(1)}, bf16[512,256]{1,0:T(8,128)(2,1)S(1)}, u32[]{:S(2)}, u32[]{:S(2)}) %collective-permute-start.8) | collective-permute-done | bytes 262176 | tf_op jit(solution)/shard_map/ppermute | solution.py:35
  63.7 2.9 %collective-permute-done.10.refs_15_ = bf16[512,256]{1,0:T(8,128)(2,1)S(1)} collective-permute-done((bf16[512,256]{1,0:T(8,128)(2,1)S(1)}, bf16[512,256]{1,0:T(8,128)(2,1)S(1)}, u32[]{:S(2)}, u32[]{:S(2)}) %collective-permute-start.10) | collective-permute-done | bytes 262176 | tf_op jit(solution)/shard_map/ppermute | solution.py:35
  72.7 3.3 %collective-permute-done.12.refs_17_ = bf16[512,256]{1,0:T(8,128)(2,1)S(1)} collective-permute-done((bf16[512,256]{1,0:T(8,128)(2,1)S(1)}, bf16[512,256]{1,0:T(8,128)(2,1)S(1)}, u32[]{:S(2)}, u32[]{:S(2)}) %collective-permute-start.12) | collective-permute-done | bytes 262176 | tf_op jit(solution)/shard_map/ppermute | solution.py:35
  85.7 2.4 %collective-permute-start.16 = (bf16[2048,256]{1,0:T(8,128)(2,1)}, bf16[2048,256]{1,0:T(8,128)(2,1)}, u32[]{:S(2)}, u32[]{:S(2)}) collective-permute-start(bf16[2048,256]{1,0:T(8,128)(2,1)} %pad_maximum_fusion), channel_id=1, source_target_pairs={{0,8},{8,0},{1,9},{9,1},{2,10},{10,2},{3,11},{11,3},{4,12},{12,4},... | collective-permute-start | bytes 3145736 | tf_op jit(solution)/shard_map/ppermute | solution.py:39
  91.0 2.7 %collective-permute-start.19 = (bf16[512,256]{1,0:T(8,128)(2,1)}, bf16[512,256]{1,0:T(8,128)(2,1)S(1)}, u32[]{:S(2)}, u32[]{:S(2)}) collective-permute-start(bf16[512,256]{1,0:T(8,128)(2,1)} %copy-done.19), channel_id=1, source_target_pairs={{0,32},{8,488},{32,64},{40,8},{64,96},{72,40},{96,128},{104,72},{1... | collective-permute-start | bytes 786440 | tf_op jit(solution)/shard_map/ppermute | solution.py:35
  93.7 5.1 %collective-permute-start.20 = (bf16[512,256]{1,0:T(8,128)(2,1)}, bf16[512,256]{1,0:T(8,128)(2,1)}, u32[]{:S(2)}, u32[]{:S(2)}) collective-permute-start(bf16[512,256]{1,0:T(8,128)(2,1)} %copy-done.20), channel_id=1, source_target_pairs={{0,32},{8,488},{32,64},{40,8},{64,96},{72,40},{96,128},{104,72},{1... | collective-permute-start | bytes 786440 | tf_op jit(solution)/shard_map/ppermute | solution.py:35
  100.7 2.9 %collective-permute-done.20.refs_25_ = bf16[512,256]{1,0:T(8,128)(2,1)} collective-permute-done((bf16[512,256]{1,0:T(8,128)(2,1)}, bf16[512,256]{1,0:T(8,128)(2,1)}, u32[]{:S(2)}, u32[]{:S(2)}) %collective-permute-start.20) | collective-permute-done | bytes 262176 | tf_op jit(solution)/shard_map/ppermute | solution.py:35
  104.8 10.2 %forward.1 = (f32[2,128,512]{2,1,0:T(8,128)S(1)}, f32[2,2688,512]{2,1,0:T(8,128)S(1)}, bf16[5504,256]{1,0:T(8,128)(2,1)S(1)}, f32[8,4,128]{2,1,0:T(4,128)S(1)}) custom-call(s32[2,21]{1,0:T(2,128)S(1)} %compare_select_fusion.7.refs_0_, s32[128]{0:T(128)S(1)} %get-tuple-element.77.refs_1_, bf16[256,512]{1,0:T(8,128)(2,1)S(1)} %copy-done, ...), custom_call_target="tpu_custom_call" | custom-call | flops 1409286144 | bytes 16777216 | tf_op jit(solution)/shard_map/forward/pallas_call | solution.py:351
  115.0 11.1 %all_to_all.5.refs_2_.refs_1_ = f32[8,4,128]{2,1,0:T(4,128)S(1)} all-to-all(f32[8,4,128]{2,1,0:T(4,128)S(1)} %get-tuple-element.40), channel_id=1, replica_groups=mesh['z'=16,'xh'=2,'core'=2,'y'=4,'xl'=2] {'y','xl'}, dimensions={0} | all-to-all | bytes 32768 | tf_op jit(solution)/shard_map/all_to_all | solution.py:89
  126.1 9.6 %backward.1 = (bf16[2,2688,512]{2,1,0:T(8,128)(2,1)S(1)}, bf16[8192,256]{1,0:T(8,128)(2,1)S(1)}, bf16[3072,256]{1,0:T(8,128)(2,1)S(1)}, bf16[2048,256]{1,0:T(8,1...) custom-call(s32[2,21]{1,0:T(2,128)S(1)} %compare_select_fusion.7.refs_0_, ...), custom_call_target="tpu_custom_call" | custom-call | flops 2113929216 | bytes 33554432 | tf_op jit(solution)/shard_map/backward/pallas_call | solution.py:372
  137.7 4.1 %collective-permute-start.22 = (bf16[512,256]{1,0:T(8,128)(2,1)S(1)}, bf16[512,256]{1,0:T(8,128)(2,1)S(1)}, u32[]{:S(2)}, u32[]{:S(2)}) collective-permute-start(bf16[512,256]{1,0:T(8,128)(2,1)S(1)} %get-tuple-element.48), channel_id=1, source_target_pairs={{0,32},{8,488},{32,64},{40,8},{64,96},{72,40},{96,128},{104,72},{1... | collective-permute-start | bytes 786440 | tf_op jit(solution)/shard_map/ppermute | solution.py:35
  143.8 3.0 %collective-permute-start.21 = (bf16[512,256]{1,0:T(8,128)(2,1)S(1)}, bf16[512,256]{1,0:T(8,128)(2,1)S(1)}, u32[]{:S(2)}, u32[]{:S(2)}) collective-permute-start(bf16[512,256]{1,0:T(8,128)(2,1)S(1)} %get-tuple-element.47), channel_id=1, source_target_pairs={{0,32},{8,488},{32,64},{40,8},{64,96},{72,40},{96,128},{104,72},{1... | collective-permute-start | bytes 786440 | tf_op jit(solution)/shard_map/ppermute | solution.py:35
  147.3 4.1 %collective-permute-start.25 = (bf16[512,256]{1,0:T(8,128)(2,1)S(1)}, bf16[512,256]{1,0:T(8,128)(2,1)S(1)}, u32[]{:S(2)}, u32[]{:S(2)}) collective-permute-start(bf16[512,256]{1,0:T(8,128)(2,1)S(1)} %add_convert_fusion.14), channel_id=1, source_target_pairs={{0,32},{8,488},{32,64},{40,8},{64,96},{72,40},{96,128},{104,72},{1... | collective-permute-start | bytes 786440 | tf_op jit(solution)/shard_map/ppermute | solution.py:35
  153.4 3.9 %collective-permute-start.24 = (bf16[512,256]{1,0:T(8,128)(2,1)S(1)}, bf16[512,256]{1,0:T(8,128)(2,1)S(1)}, u32[]{:S(2)}, u32[]{:S(2)}) collective-permute-start(bf16[512,256]{1,0:T(8,128)(2,1)S(1)} %add_convert_fusion.13), channel_id=1, source_target_pairs={{0,32},{8,488},{32,64},{40,8},{64,96},{72,40},{96,128},{104,72},{1... | collective-permute-start | bytes 786440 | tf_op jit(solution)/shard_map/ppermute | solution.py:35
  157.5 3.4 %collective-permute-start.27 = (bf16[512,256]{1,0:T(8,128)(2,1)S(1)}, bf16[512,256]{1,0:T(8,128)(2,1)S(1)}, u32[]{:S(2)}, u32[]{:S(2)}) collective-permute-start(bf16[512,256]{1,0:T(8,128)(2,1)S(1)} %add_convert_fusion.12), channel_id=1, source_target_pairs={{0,32},{8,488},{32,64},{40,8},{64,96},{72,40},{96,128},{104,72},{1... | collective-permute-start | bytes 786440 | tf_op jit(solution)/shard_map/ppermute | solution.py:35
  163.0 2.7 %collective-permute-start.26 = (bf16[512,256]{1,0:T(8,128)(2,1)S(1)}, bf16[512,256]{1,0:T(8,128)(2,1)S(1)}, u32[]{:S(2)}, u32[]{:S(2)}) collective-permute-start(bf16[512,256]{1,0:T(8,128)(2,1)S(1)} %add_convert_fusion.11), channel_id=1, source_target_pairs={{0,32},{8,488},{32,64},{40,8},{64,96},{72,40},{96,128},{104,72},{1... | collective-permute-start | bytes 786440 | tf_op jit(solution)/shard_map/ppermute | solution.py:35
  167.1 2.2 collective-permute-start.30
  169.2 3.3 %collective-permute-done.26 = bf16[512,256]{1,0:T(8,128)(2,1)S(1)} collective-permute-done((bf16[512,256]{1,0:T(8,128)(2,1)S(1)}, bf16[512,256]{1,0:T(8,128)(2,1)S(1)}, u32[]{:S(2)}, u32[]{:S(2)}) %collective-permute-start.26) | collective-permute-done | bytes 262176 | tf_op jit(solution)/shard_map/ppermute | solution.py:35
  178.6 3.5 %collective-permute-done.29 = bf16[512,256]{1,0:T(8,128)(2,1)S(1)} collective-permute-done((bf16[512,256]{1,0:T(8,128)(2,1)S(1)}, bf16[512,256]{1,0:T(8,128)(2,1)S(1)}, u32[]{:S(2)}, u32[]{:S(2)}) %collective-permute-start.29) | collective-permute-done | bytes 262176 | tf_op jit(solution)/shard_map/ppermute | solution.py:35
  188.2 3.5 %collective-permute-done.31 = bf16[512,256]{1,0:T(8,128)(2,1)S(1)} collective-permute-done((bf16[512,256]{1,0:T(8,128)(2,1)S(1)}, bf16[512,256]{1,0:T(8,128)(2,1)S(1)}, u32[]{:S(2)}, u32[]{:S(2)}) %collective-permute-start.31) | collective-permute-done | bytes 262176 | tf_op jit(solution)/shard_map/ppermute | solution.py:35
  197.8 3.5 %collective-permute-done.34 = bf16[512,256]{1,0:T(8,128)(2,1)S(1)} collective-permute-done((bf16[512,256]{1,0:T(8,128)(2,1)S(1)}, bf16[512,256]{1,0:T(8,128)(2,1)S(1)}, u32[]{:S(2)}, u32[]{:S(2)}) %collective-permute-start.34) | collective-permute-done | bytes 262176 | tf_op jit(solution)/shard_map/ppermute | solution.py:35
  207.4 3.5 %collective-permute-done.36 = bf16[512,256]{1,0:T(8,128)(2,1)S(1)} collective-permute-done((bf16[512,256]{1,0:T(8,128)(2,1)S(1)}, bf16[512,256]{1,0:T(8,128)(2,1)S(1)}, u32[]{:S(2)}, u32[]{:S(2)}) %collective-permute-start.36) | collective-permute-done | bytes 262176 | tf_op jit(solution)/shard_map/ppermute | solution.py:35
  216.9 3.5 %collective-permute-done.38 = bf16[512,256]{1,0:T(8,128)(2,1)S(1)} collective-permute-done((bf16[512,256]{1,0:T(8,128)(2,1)S(1)}, bf16[512,256]{1,0:T(8,128)(2,1)S(1)}, u32[]{:S(2)}, u32[]{:S(2)}) %collective-permute-start.38) | collective-permute-done | bytes 262176 | tf_op jit(solution)/shard_map/ppermute | solution.py:35
  220.6 2.8 %collective-permute-start.41 = (bf16[256,256]{1,0:T(8,128)(2,1)S(1)}, bf16[256,256]{1,0:T(8,128)(2,1)S(1)}, u32[]{:S(2)}, u32[]{:S(2)}) collective-permute-start(bf16[256,256]{1,0:T(8,128)(2,1)S(1)} %slice.182), channel_id=1, source_target_pairs={{0,16},{16,0},{1,17},{17,1},{2,18},{18,2},{3,19},{19,3},{4,20},{20... | collective-permute-start | bytes 393224 | tf_op jit(solution)/shard_map/ppermute | solution.py:84
  223.3 2.3 %finish.1 = (bf16[256,512]{1,0:T(8,128)(2,1)}, bf16[256,512]{1,0:T(8,128)(2,1)}) custom-call(s32[2,21]{1,0:T(2,128)S(1)} %compare_select_fusion.7.refs_0_, f32[8,4,128]{2,1,0:T(4,128)S(1)} %all_to_all.5.refs_2_.refs_1_, f32[1,512]{1,0:T(1,128)S(1)} %bitcast.3, f32[2,128,512]{2,1,0:T(8,128)S(1)} %get-tuple-element.41.refs_6_.refs_3_, ...), custom_call_target="tpu_custom_call" | custom-call | flops 704643072 | bytes 8388608 | tf_op jit(solution)/shard_map/finish/pallas_call | solution.py:391
  225.7 3.2 %collective-permute-done.41 = bf16[256,256]{1,0:T(8,128)(2,1)S(1)} collective-permute-done((bf16[256,256]{1,0:T(8,128)(2,1)S(1)}, bf16[256,256]{1,0:T(8,128)(2,1)S(1)}, u32[]{:S(2)}, u32[]{:S(2)}) %collective-permute-start.41) | collective-permute-done | bytes 131104 | tf_op jit(solution)/shard_map/ppermute | solution.py:84
  (149 shorter events, 90.8 us)
Async XLA Ops:
  2.3 10.7 %collective-permute-start = (bf16[256,256]{1,0:T(8,128)(2,1)S(1)}, bf16[256,256]{1,0:T(8,128)(2,1)S(1)}, u32[]{:S(2)}, u32[]{:S(2)}) collective-permute-start(bf16[256,256]{1,0:T(8,128)(2,1)S(1)} %constant_dynamic-update-slice_fusion), channel_id=1, source_target_pairs={{0,16},{16,0},{1,17},{17,1},{2,18},{18,2},{3,19},{19,3},{4,20},{20... | collective-permute-start | bytes 393224 | tf_op jit(solution)/shard_map/ppermute | solution.py:43
  15.0 13.7 %collective-permute-start.2 = (bf16[512,256]{1,0:T(8,128)(2,1)S(1)}, bf16[512,256]{1,0:T(8,128)(2,1)S(1)}, u32[]{:S(2)}, u32[]{:S(2)}) collective-permute-start(bf16[512,256]{1,0:T(8,128)(2,1)S(1)} %pad_maximum_fusion.2.refs_5_), channel_id=1, source_target_pairs={{0,32},{8,488},{32,64},{40,8},{64,96},{72,40},{96,128},{104,72},{1... | collective-permute-start | bytes 786440 | tf_op jit(solution)/shard_map/ppermute | solution.py:35
  17.0 14.5 %collective-permute-start.3 = (bf16[512,256]{1,0:T(8,128)(2,1)S(1)}, bf16[512,256]{1,0:T(8,128)(2,1)S(1)}, u32[]{:S(2)}, u32[]{:S(2)}) collective-permute-start(bf16[512,256]{1,0:T(8,128)(2,1)S(1)} %collective-permute-done.1.refs_6_), channel_id=1, source_target_pairs={{0,32},{8,488},{32,64},{40,8},{64,96},{72,40},{96,128},{104,72},{1... | collective-permute-start | bytes 786440 | tf_op jit(solution)/shard_map/ppermute | solution.py:35
  28.7 9.5 %collective-permute-start.4 = (bf16[512,256]{1,0:T(8,128)(2,1)S(1)}, bf16[512,256]{1,0:T(8,128)(2,1)S(1)}, u32[]{:S(2)}, u32[]{:S(2)}) collective-permute-start(bf16[512,256]{1,0:T(8,128)(2,1)S(1)} %collective-permute-done.2.refs_7_), channel_id=1, source_target_pairs={{0,32},{8,488},{32,64},{40,8},{64,96},{72,40},{96,128},{104,72},{1... | collective-permute-start | bytes 786440 | tf_op jit(solution)/shard_map/ppermute | solution.py:35
  31.5 9.5 %collective-permute-start.5 = (bf16[512,256]{1,0:T(8,128)(2,1)S(1)}, bf16[512,256]{1,0:T(8,128)(2,1)S(1)}, u32[]{:S(2)}, u32[]{:S(2)}) collective-permute-start(bf16[512,256]{1,0:T(8,128)(2,1)S(1)} %collective-permute-done.3.refs_8_), channel_id=1, source_target_pairs={{0,32},{8,488},{32,64},{40,8},{64,96},{72,40},{96,128},{104,72},{1... | collective-permute-start | bytes 786440 | tf_op jit(solution)/shard_map/ppermute | solution.py:35
  38.2 9.5 %collective-permute-start.6 = (bf16[512,256]{1,0:T(8,128)(2,1)S(1)}, bf16[512,256]{1,0:T(8,128)(2,1)S(1)}, u32[]{:S(2)}, u32[]{:S(2)}) collective-permute-start(bf16[512,256]{1,0:T(8,128)(2,1)S(1)} %collective-permute-done.4.refs_9_), channel_id=1, source_target_pairs={{0,32},{8,488},{32,64},{40,8},{64,96},{72,40},{96,128},{104,72},{1... | collective-permute-start | bytes 786440 | tf_op jit(solution)/shard_map/ppermute | solution.py:35
  41.0 9.5 %collective-permute-start.7 = (bf16[512,256]{1,0:T(8,128)(2,1)S(1)}, bf16[512,256]{1,0:T(8,128)(2,1)S(1)}, u32[]{:S(2)}, u32[]{:S(2)}) collective-permute-start(bf16[512,256]{1,0:T(8,128)(2,1)S(1)} %collective-permute-done.5.refs_10_), channel_id=1, source_target_pairs={{0,32},{8,488},{32,64},{40,8},{64,96},{72,40},{96,128},{104,72},{1... | collective-permute-start | bytes 786440 | tf_op jit(solution)/shard_map/ppermute | solution.py:35
  76.0 12.1 %collective-permute-start.14 = (bf16[512,256]{1,0:T(8,128)(2,1)S(1)}, bf16[512,256]{1,0:T(8,128)(2,1)S(1)}, u32[]{:S(2)}, u32[]{:S(2)}) collective-permute-start(bf16[512,256]{1,0:T(8,128)(2,1)S(1)} %collective-permute-done.12.refs_17_), channel_id=1, source_target_pairs={{0,32},{8,488},{32,64},{40,8},{64,96},{72,40},{96,128},{104,72},{1... | collective-permute-start | bytes 786440 | tf_op jit(solution)/shard_map/ppermute | solution.py:35
  81.5 22.1 %collective-permute-start.17 = (bf16[3072,256]{1,0:T(8,128)(2,1)}, bf16[3072,256]{1,0:T(8,128)(2,1)S(1)}, u32[]{:S(2)}, u32[]{:S(2)}) collective-permute-start(bf16[3072,256]{1,0:T(8,128)(2,1)} %constant_dynamic-update-slice_fusion.2), channel_id=1, source_target_pairs={{0,8},{8,0},{1,9},{9,1},{2,10},{10,2},{3,11},{11,3},{4,12},{12,4},... | collective-permute-start | bytes 4718600 | tf_op jit(solution)/shard_map/ppermute | solution.py:39
  85.7 13.3 %collective-permute-start.16 = (bf16[2048,256]{1,0:T(8,128)(2,1)}, bf16[2048,256]{1,0:T(8,128)(2,1)}, u32[]{:S(2)}, u32[]{:S(2)}) collective-permute-start(bf16[2048,256]{1,0:T(8,128)(2,1)} %pad_maximum_fusion), channel_id=1, source_target_pairs={{0,8},{8,0},{1,9},{9,1},{2,10},{10,2},{3,11},{11,3},{4,12},{12,4},... | collective-permute-start | bytes 3145736 | tf_op jit(solution)/shard_map/ppermute | solution.py:39
  88.4 15.2 %collective-permute-start.18 = (bf16[2048,256]{1,0:T(8,128)(2,1)S(1)}, bf16[2048,256]{1,0:T(8,128)(2,1)}, u32[]{:S(2)}, u32[]{:S(2)}) collective-permute-start(bf16[2048,256]{1,0:T(8,128)(2,1)S(1)} %pad_maximum_fusion.1), channel_id=1, source_target_pairs={{0,8},{8,0},{1,9},{9,1},{2,10},{10,2},{3,11},{11,3},{4,12},{12,4},... | collective-permute-start | bytes 3145736 | tf_op jit(solution)/shard_map/ppermute | solution.py:39
  91.0 9.7 %collective-permute-start.19 = (bf16[512,256]{1,0:T(8,128)(2,1)}, bf16[512,256]{1,0:T(8,128)(2,1)S(1)}, u32[]{:S(2)}, u32[]{:S(2)}) collective-permute-start(bf16[512,256]{1,0:T(8,128)(2,1)} %copy-done.19), channel_id=1, source_target_pairs={{0,32},{8,488},{32,64},{40,8},{64,96},{72,40},{96,128},{104,72},{1... | collective-permute-start | bytes 786440 | tf_op jit(solution)/shard_map/ppermute | solution.py:35
  93.7 9.9 %collective-permute-start.20 = (bf16[512,256]{1,0:T(8,128)(2,1)}, bf16[512,256]{1,0:T(8,128)(2,1)}, u32[]{:S(2)}, u32[]{:S(2)}) collective-permute-start(bf16[512,256]{1,0:T(8,128)(2,1)} %copy-done.20), channel_id=1, source_target_pairs={{0,32},{8,488},{32,64},{40,8},{64,96},{72,40},{96,128},{104,72},{1... | collective-permute-start | bytes 786440 | tf_op jit(solution)/shard_map/ppermute | solution.py:35
  135.8 11.4 %collective-permute-start.23 = (bf16[2048,256]{1,0:T(8,128)(2,1)S(1)}, bf16[2048,256]{1,0:T(8,128)(2,1)S(1)}, u32[]{:S(2)}, u32[]{:S(2)}) collective-permute-start(bf16[2048,256]{1,0:T(8,128)(2,1)S(1)} %get-tuple-element.50), channel_id=1, source_target_pairs={{0,8},{8,0},{1,9},{9,1},{2,10},{10,2},{3,11},{11,3},{4,12},{12,4},... | collective-permute-start | bytes 3145736 | tf_op jit(solution)/shard_map/ppermute | solution.py:39
  137.7 9.5 %collective-permute-start.22 = (bf16[512,256]{1,0:T(8,128)(2,1)S(1)}, bf16[512,256]{1,0:T(8,128)(2,1)S(1)}, u32[]{:S(2)}, u32[]{:S(2)}) collective-permute-start(bf16[512,256]{1,0:T(8,128)(2,1)S(1)} %get-tuple-element.48), channel_id=1, source_target_pairs={{0,32},{8,488},{32,64},{40,8},{64,96},{72,40},{96,128},{104,72},{1... | collective-permute-start | bytes 786440 | tf_op jit(solution)/shard_map/ppermute | solution.py:35
  141.8 23.9 %collective-permute-start.28 = (bf16[2048,256]{1,0:T(8,128)(2,1)S(1)}, bf16[2048,256]{1,0:T(8,128)(2,1)S(1)}, u32[]{:S(2)}, u32[]{:S(2)}) collective-permute-start(bf16[2048,256]{1,0:T(8,128)(2,1)S(1)} %get-tuple-element.57), channel_id=1, source_target_pairs={{0,8},{8,0},{1,9},{9,1},{2,10},{10,2},{3,11},{11,3},{4,12},{12,4},... | collective-permute-start | bytes 3145736 | tf_op jit(solution)/shard_map/ppermute | solution.py:39
  143.8 9.5 %collective-permute-start.21 = (bf16[512,256]{1,0:T(8,128)(2,1)S(1)}, bf16[512,256]{1,0:T(8,128)(2,1)S(1)}, u32[]{:S(2)}, u32[]{:S(2)}) collective-permute-start(bf16[512,256]{1,0:T(8,128)(2,1)S(1)} %get-tuple-element.47), channel_id=1, source_target_pairs={{0,32},{8,488},{32,64},{40,8},{64,96},{72,40},{96,128},{104,72},{1... | collective-permute-start | bytes 786440 | tf_op jit(solution)/shard_map/ppermute | solution.py:35
  147.3 10.1 %collective-permute-start.25 = (bf16[512,256]{1,0:T(8,128)(2,1)S(1)}, bf16[512,256]{1,0:T(8,128)(2,1)S(1)}, u32[]{:S(2)}, u32[]{:S(2)}) collective-permute-start(bf16[512,256]{1,0:T(8,128)(2,1)S(1)} %add_convert_fusion.14), channel_id=1, source_target_pairs={{0,32},{8,488},{32,64},{40,8},{64,96},{72,40},{96,128},{104,72},{1... | collective-permute-start | bytes 786440 | tf_op jit(solution)/shard_map/ppermute | solution.py:35
  151.4 32.8 %collective-permute-start.33 = (bf16[3072,256]{1,0:T(8,128)(2,1)S(1)}, bf16[3072,256]{1,0:T(8,128)(2,1)S(1)}, u32[]{:S(2)}, u32[]{:S(2)}) collective-permute-start(bf16[3072,256]{1,0:T(8,128)(2,1)S(1)} %get-tuple-element.64), channel_id=1, source_target_pairs={{0,8},{8,0},{1,9},{9,1},{2,10},{10,2},{3,11},{11,3},{4,12},{12,4},... | collective-permute-start | bytes 4718600 | tf_op jit(solution)/shard_map/ppermute | solution.py:39
  153.4 9.5 %collective-permute-start.24 = (bf16[512,256]{1,0:T(8,128)(2,1)S(1)}, bf16[512,256]{1,0:T(8,128)(2,1)S(1)}, u32[]{:S(2)}, u32[]{:S(2)}) collective-permute-start(bf16[512,256]{1,0:T(8,128)(2,1)S(1)} %add_convert_fusion.13), channel_id=1, source_target_pairs={{0,32},{8,488},{32,64},{40,8},{64,96},{72,40},{96,128},{104,72},{1... | collective-permute-start | bytes 786440 | tf_op jit(solution)/shard_map/ppermute | solution.py:35
  157.5 9.5 %collective-permute-start.27 = (bf16[512,256]{1,0:T(8,128)(2,1)S(1)}, bf16[512,256]{1,0:T(8,128)(2,1)S(1)}, u32[]{:S(2)}, u32[]{:S(2)}) collective-permute-start(bf16[512,256]{1,0:T(8,128)(2,1)S(1)} %add_convert_fusion.12), channel_id=1, source_target_pairs={{0,32},{8,488},{32,64},{40,8},{64,96},{72,40},{96,128},{104,72},{1... | collective-permute-start | bytes 786440 | tf_op jit(solution)/shard_map/ppermute | solution.py:35
  163.0 9.5 %collective-permute-start.26 = (bf16[512,256]{1,0:T(8,128)(2,1)S(1)}, bf16[512,256]{1,0:T(8,128)(2,1)S(1)}, u32[]{:S(2)}, u32[]{:S(2)}) collective-permute-start(bf16[512,256]{1,0:T(8,128)(2,1)S(1)} %add_convert_fusion.11), channel_id=1, source_target_pairs={{0,32},{8,488},{32,64},{40,8},{64,96},{72,40},{96,128},{104,72},{1... | collective-permute-start | bytes 786440 | tf_op jit(solution)/shard_map/ppermute | solution.py:35
  167.1 9.5 %collective-permute-start.30 = (bf16[512,256]{1,0:T(8,128)(2,1)S(1)}, bf16[512,256]{1,0:T(8,128)(2,1)S(1)}, u32[]{:S(2)}, u32[]{:S(2)}) collective-permute-start(bf16[512,256]{1,0:T(8,128)(2,1)S(1)} %add_convert_fusion.10), channel_id=1, source_target_pairs={{0,32},{8,488},{32,64},{40,8},{64,96},{72,40},{96,128},{104,72},{1... | collective-permute-start | bytes 786440 | tf_op jit(solution)/shard_map/ppermute | solution.py:35
  172.6 9.5 %collective-permute-start.29 = (bf16[512,256]{1,0:T(8,128)(2,1)S(1)}, bf16[512,256]{1,0:T(8,128)(2,1)S(1)}, u32[]{:S(2)}, u32[]{:S(2)}) collective-permute-start(bf16[512,256]{1,0:T(8,128)(2,1)S(1)} %add_convert_fusion.9), channel_id=1, source_target_pairs={{0,32},{8,488},{32,64},{40,8},{64,96},{72,40},{96,128},{104,72},{1... | collective-permute-start | bytes 786440 | tf_op jit(solution)/shard_map/ppermute | solution.py:35
  176.7 9.5 %collective-permute-start.32 = (bf16[512,256]{1,0:T(8,128)(2,1)S(1)}, bf16[512,256]{1,0:T(8,128)(2,1)S(1)}, u32[]{:S(2)}, u32[]{:S(2)}) collective-permute-start(bf16[512,256]{1,0:T(8,128)(2,1)S(1)} %add_convert_fusion.8), channel_id=1, source_target_pairs={{0,32},{8,488},{32,64},{40,8},{64,96},{72,40},{96,128},{104,72},{1... | collective-permute-start | bytes 786440 | tf_op jit(solution)/shard_map/ppermute | solution.py:35
  182.2 9.5 %collective-permute-start.31 = (bf16[512,256]{1,0:T(8,128)(2,1)S(1)}, bf16[512,256]{1,0:T(8,128)(2,1)S(1)}, u32[]{:S(2)}, u32[]{:S(2)}) collective-permute-start(bf16[512,256]{1,0:T(8,128)(2,1)S(1)} %add_convert_fusion.7), channel_id=1, source_target_pairs={{0,32},{8,488},{32,64},{40,8},{64,96},{72,40},{96,128},{104,72},{1... | collective-permute-start | bytes 786440 | tf_op jit(solution)/shard_map/ppermute | solution.py:35
  186.2 9.5 %collective-permute-start.35 = (bf16[512,256]{1,0:T(8,128)(2,1)S(1)}, bf16[512,256]{1,0:T(8,128)(2,1)S(1)}, u32[]{:S(2)}, u32[]{:S(2)}) collective-permute-start(bf16[512,256]{1,0:T(8,128)(2,1)S(1)} %add_convert_fusion.6), channel_id=1, source_target_pairs={{0,32},{8,488},{32,64},{40,8},{64,96},{72,40},{96,128},{104,72},{1... | collective-permute-start | bytes 786440 | tf_op jit(solution)/shard_map/ppermute | solution.py:35
  191.8 9.5 %collective-permute-start.34 = (bf16[512,256]{1,0:T(8,128)(2,1)S(1)}, bf16[512,256]{1,0:T(8,128)(2,1)S(1)}, u32[]{:S(2)}, u32[]{:S(2)}) collective-permute-start(bf16[512,256]{1,0:T(8,128)(2,1)S(1)} %add_convert_fusion.5), channel_id=1, source_target_pairs={{0,32},{8,488},{32,64},{40,8},{64,96},{72,40},{96,128},{104,72},{1... | collective-permute-start | bytes 786440 | tf_op jit(solution)/shard_map/ppermute | solution.py:35
  195.8 9.5 %collective-permute-start.37 = (bf16[512,256]{1,0:T(8,128)(2,1)S(1)}, bf16[512,256]{1,0:T(8,128)(2,1)S(1)}, u32[]{:S(2)}, u32[]{:S(2)}) collective-permute-start(bf16[512,256]{1,0:T(8,128)(2,1)S(1)} %add_convert_fusion.4), channel_id=1, source_target_pairs={{0,32},{8,488},{32,64},{40,8},{64,96},{72,40},{96,128},{104,72},{1... | collective-permute-start | bytes 786440 | tf_op jit(solution)/shard_map/ppermute | solution.py:35
  201.4 9.5 %collective-permute-start.36 = (bf16[512,256]{1,0:T(8,128)(2,1)S(1)}, bf16[512,256]{1,0:T(8,128)(2,1)S(1)}, u32[]{:S(2)}, u32[]{:S(2)}) collective-permute-start(bf16[512,256]{1,0:T(8,128)(2,1)S(1)} %add_convert_fusion.3), channel_id=1, source_target_pairs={{0,32},{8,488},{32,64},{40,8},{64,96},{72,40},{96,128},{104,72},{1... | collective-permute-start | bytes 786440 | tf_op jit(solution)/shard_map/ppermute | solution.py:35
  205.4 9.5 %collective-permute-start.39 = (bf16[512,256]{1,0:T(8,128)(2,1)S(1)}, bf16[512,256]{1,0:T(8,128)(2,1)S(1)}, u32[]{:S(2)}, u32[]{:S(2)}) collective-permute-start(bf16[512,256]{1,0:T(8,128)(2,1)S(1)} %add_convert_fusion.2), channel_id=1, source_target_pairs={{0,32},{8,488},{32,64},{40,8},{64,96},{72,40},{96,128},{104,72},{1... | collective-permute-start | bytes 786440 | tf_op jit(solution)/shard_map/ppermute | solution.py:35
  211.0 9.5 %collective-permute-start.38 = (bf16[512,256]{1,0:T(8,128)(2,1)S(1)}, bf16[512,256]{1,0:T(8,128)(2,1)S(1)}, u32[]{:S(2)}, u32[]{:S(2)}) collective-permute-start(bf16[512,256]{1,0:T(8,128)(2,1)S(1)} %add_convert_fusion.1), channel_id=1, source_target_pairs={{0,32},{8,488},{32,64},{40,8},{64,96},{72,40},{96,128},{104,72},{1... | collective-permute-start | bytes 786440 | tf_op jit(solution)/shard_map/ppermute | solution.py:35
  (33 other events, 587.9 us)

commit v3 on v2

--- a/solution.py
+++ b/solution.py
@@ -40,8 +40,12 @@
 
 
 def gather_blocks(kv):
-    pair = jnp.concatenate([kv, lax.ppermute(kv, "xh", SWAP)], axis=0)
-    own, other = pair, swap(pair)
+    core = lax.axis_index("core")
+    four = lax.all_gather(kv, ("xh", "core")).reshape(2, 2, *kv.shape)
+    own, other = (
+        lax.dynamic_index_in_dim(four, c, 1, keepdims=False).reshape(PART, kv.shape[1])
+        for c in (core, 1 - core)
+    )
     chunk, mine, theirs = [own, other], [], []
     waiting = []
     for s in range(1, HALF):
@@ -52,6 +56,12 @@
             theirs.append(swap(jnp.concatenate(waiting, axis=0)))
             waiting = []
     return chunk + mine + theirs + [ring(own), ring(other)]
+
+
+def beside(a, b):
+    none, width = (0, 0, 0), (0, a.shape[1], 0)
+    zero = jnp.zeros((), a.dtype)
+    return lax.pad(a, zero, (none, width)) + lax.pad(b, zero, (none, width[1::-1] + (0,)))
 
 
 def total(*terms):
@@ -81,8 +91,11 @@
     other, mine = lax.optimization_barrier((other, mine))
     own = ring(own)
     own = total(own, part_of(mine, 0), swap(other))
-    mate = lax.ppermute(own[rows:].astype(BF16), "xh", SWAP)
-    return total(own[:rows], mate)
+    first = lax.axis_index("xh") == 0
+    low, high = own[:rows], own[rows:]
+    give = jnp.where(first, high, low).astype(BF16)
+    pair = lax.all_gather(give, "xh")
+    return total(jnp.where(first, low, high), jnp.where(first, pair[1], pair[0]))
 
 
 def head_copies(x):
@@ -105,7 +118,7 @@
     owner, half = store // per_device, store % per_device
     oz, oxh, ocore = owner // 4, (owner // 2) % 2, owner % 2
     dz = (oz - z + HALF) % NZ - HALF
-    inner = (oxh ^ xh) * 2 + half
+    inner = oxh * 2 + half
     dist = jnp.abs(dz)
 
     across = ocore ^ core
@@ -153,7 +166,7 @@
             visit(k, i, base + i)
             return carry
 
-        lax.fori_loop(0, 4 * n, one, 0)
+        lax.fori_loop(0, 4 * n, one, 0, unroll=4)
         base += 4 * n
 
 
@@ -403,7 +416,7 @@
     key_width = keys.shape[1]
     heads = lax.axis_size(HEAD)
     gain = gain.reshape(1, queries.shape[1])
-    gathered = gather_blocks(jnp.concatenate([keys, values], axis=1))
+    gathered = gather_blocks(beside(keys, values))
     slots, source_of, back_of = positions(key_blocks, span_order, queries.shape[0] // BLOCK)
     attended, weights, held, sums = forward(
         heads, slots, source_of, queries, cotangent, gain, gathered

time: 231 us -> 236 us (1.022)
  the two profiles are of different devices: /device:TPU:4 before, /device:TPU:1 now
where the time goes in v3:
time: 236 us; the launch traced here: 235 us
  starting transfers between devices  146 us (62%)
  blocking collectives  31.4 us (13%)
  Pallas kernels  21.2 us (9%)
  local copies, waits for them, and re-layouts  14.3 us (6%)
  other arithmetic  10.1 us (4%)
  waiting for transfers between devices  9.81 us (4%)
    ppermute x32, starting transfers between devices, ring(): return lax.ppermute(x, RING, ring_pairs())  116 us
    ppermute x7, starting transfers between devices, swap(): return lax.ppermute(x, 'core', SWAP)  30.5 us
    all_gather x1, blocking collectives, gather_blocks(): four = lax.all_gather(kv, ('xh', 'core')).reshape(2, 2, *kv.shape)  14.7 us
    unnamed x57, local copies, waits for them, and re-layouts  11.7 us
    pallas_call x1, Pallas kernels, forward(): pl.pallas_call(lambda *refs: forward_kernel(pairs, 1.0 / math.sqrt(DH), m...  9.9 us
    ppermute x32, waiting for transfers between devices, ring(): return lax.ppermute(x, RING, ring_pairs())  9.79 us
    all_to_all x1, blocking collectives, head_copies(): return lax.all_to_all(x, HEAD, 0, 0, tiled=True)  9.56 us
    pallas_call x1, Pallas kernels, backward(): pl.pallas_call(lambda *refs: backward_kernel(pairs, 1.0 / math.sqrt(DH),...  9.01 us
  transfers between devices with their start and end apart: 39, of which 10 were waited for; matrix products, arithmetic and copies ran while one was open for 6% of the time, Pallas kernels for 1%

profile of v3, /device:TPU:1, one launch (start us, length us, event | category | flops | bytes accessed | tf_op | source)
XLA Modules:
  0.0 234.7 jit_solution(10755405010376762118)
XLA Ops:
  1.5 14.7 %all-gather = bf16[1024,256]{1,0:T(8,128)(2,1)S(1)} all-gather(bf16[256,256]{1,0:T(8,128)(2,1)S(1)} %pad_add_fusion), channel_id=2, replica_groups=mesh['z'=16,'xh'=2,'core'=2,'y'=4,'xl'=2] {'xh','core'}, dimensions={0}, use_global_device_ids=true | all-gather | bytes 655360 | tf_op jit(solution)/shard_map/all_gather | solution.py:44
  16.3 6.5 %collective-permute-start = (bf16[512,256]{1,0:T(8,128)(2,1)S(1)}, bf16[512,256]{1,0:T(8,128)(2,1)S(1)}, u32[]{:S(2)}, u32[]{:S(2)}) collective-permute-start(bf16[512,256]{1,0:T(8,128)(2,1)S(1)} %bitcast.14), channel_id=1, source_target_pairs={{0,32},{8,488},{32,64},{40,8},{64,96},{72,40},{96,128},{104,72},{1... | collective-permute-start | bytes 786440 | tf_op jit(solution)/shard_map/ppermute | solution.py:35
  26.1 5.0 %collective-permute-start.2 = (bf16[512,256]{1,0:T(8,128)(2,1)S(1)}, bf16[512,256]{1,0:T(8,128)(2,1)S(1)}, u32[]{:S(2)}, u32[]{:S(2)}) collective-permute-start(bf16[512,256]{1,0:T(8,128)(2,1)S(1)} %collective-permute-done.refs_7_), channel_id=1, source_target_pairs={{0,32},{8,488},{32,64},{40,8},{64,96},{72,40},{96,128},{104,72},{1... | collective-permute-start | bytes 786440 | tf_op jit(solution)/shard_map/ppermute | solution.py:35
  31.1 2.8 %collective-permute-start.3 = (bf16[512,256]{1,0:T(8,128)(2,1)S(1)}, bf16[512,256]{1,0:T(8,128)(2,1)S(1)}, u32[]{:S(2)}, u32[]{:S(2)}) collective-permute-start(bf16[512,256]{1,0:T(8,128)(2,1)S(1)} %collective-permute-done.1.refs_8_), channel_id=1, source_target_pairs={{0,32},{8,488},{32,64},{40,8},{64,96},{72,40},{96,128},{104,72},{1... | collective-permute-start | bytes 786440 | tf_op jit(solution)/shard_map/ppermute | solution.py:35
  34.4 5.0 %collective-permute-start.4 = (bf16[512,256]{1,0:T(8,128)(2,1)S(1)}, bf16[512,256]{1,0:T(8,128)(2,1)S(1)}, u32[]{:S(2)}, u32[]{:S(2)}) collective-permute-start(bf16[512,256]{1,0:T(8,128)(2,1)S(1)} %collective-permute-done.2.refs_9_), channel_id=1, source_target_pairs={{0,32},{8,488},{32,64},{40,8},{64,96},{72,40},{96,128},{104,72},{1... | collective-permute-start | bytes 786440 | tf_op jit(solution)/shard_map/ppermute | solution.py:35
  39.4 2.8 %collective-permute-start.5 = (bf16[512,256]{1,0:T(8,128)(2,1)S(1)}, bf16[512,256]{1,0:T(8,128)(2,1)S(1)}, u32[]{:S(2)}, u32[]{:S(2)}) collective-permute-start(bf16[512,256]{1,0:T(8,128)(2,1)S(1)} %collective-permute-done.3.refs_10_), channel_id=1, source_target_pairs={{0,32},{8,488},{32,64},{40,8},{64,96},{72,40},{96,128},{104,72},{1... | collective-permute-start | bytes 786440 | tf_op jit(solution)/shard_map/ppermute | solution.py:35
  43.0 4.7 %collective-permute-start.6 = (bf16[512,256]{1,0:T(8,128)(2,1)S(1)}, bf16[512,256]{1,0:T(8,128)(2,1)S(1)}, u32[]{:S(2)}, u32[]{:S(2)}) collective-permute-start(bf16[512,256]{1,0:T(8,128)(2,1)S(1)} %collective-permute-done.4.refs_11_), channel_id=1, source_target_pairs={{0,32},{8,488},{32,64},{40,8},{64,96},{72,40},{96,128},{104,72},{1... | collective-permute-start | bytes 786440 | tf_op jit(solution)/shard_map/ppermute | solution.py:35
  51.8 4.2 %collective-permute-start.8 = (bf16[512,256]{1,0:T(8,128)(2,1)S(1)}, bf16[512,256]{1,0:T(8,128)(2,1)S(1)}, u32[]{:S(2)}, u32[]{:S(2)}) collective-permute-start(bf16[512,256]{1,0:T(8,128)(2,1)S(1)} %collective-permute-done.6.refs_13_), channel_id=1, source_target_pairs={{0,32},{8,488},{32,64},{40,8},{64,96},{72,40},{96,128},{104,72},{1... | collective-permute-start | bytes 786440 | tf_op jit(solution)/shard_map/ppermute | solution.py:35
  56.0 2.8 %collective-permute-start.9 = (bf16[512,256]{1,0:T(8,128)(2,1)S(1)}, bf16[512,256]{1,0:T(8,128)(2,1)S(1)}, u32[]{:S(2)}, u32[]{:S(2)}) collective-permute-start(bf16[512,256]{1,0:T(8,128)(2,1)S(1)} %collective-permute-done.7.refs_14_), channel_id=1, source_target_pairs={{0,32},{8,488},{32,64},{40,8},{64,96},{72,40},{96,128},{104,72},{1... | collective-permute-start | bytes 786440 | tf_op jit(solution)/shard_map/ppermute | solution.py:35
  61.4 2.9 %collective-permute-start.10 = (bf16[512,256]{1,0:T(8,128)(2,1)S(1)}, bf16[512,256]{1,0:T(8,128)(2,1)S(1)}, u32[]{:S(2)}, u32[]{:S(2)}) collective-permute-start(bf16[512,256]{1,0:T(8,128)(2,1)S(1)} %collective-permute-done.8.refs_15_), channel_id=1, source_target_pairs={{0,32},{8,488},{32,64},{40,8},{64,96},{72,40},{96,128},{104,72},{1... | collective-permute-start | bytes 786440 | tf_op jit(solution)/shard_map/ppermute | solution.py:35
  64.4 2.8 %collective-permute-start.11 = (bf16[512,256]{1,0:T(8,128)(2,1)S(1)}, bf16[512,256]{1,0:T(8,128)(2,1)S(1)}, u32[]{:S(2)}, u32[]{:S(2)}) collective-permute-start(bf16[512,256]{1,0:T(8,128)(2,1)S(1)} %collective-permute-done.9.refs_16_), channel_id=1, source_target_pairs={{0,32},{8,488},{32,64},{40,8},{64,96},{72,40},{96,128},{104,72},{1... | collective-permute-start | bytes 786440 | tf_op jit(solution)/shard_map/ppermute | solution.py:35
  69.3 3.3 %collective-permute-start.12 = (bf16[512,256]{1,0:T(8,128)(2,1)S(1)}, bf16[512,256]{1,0:T(8,128)(2,1)}, u32[]{:S(2)}, u32[]{:S(2)}) collective-permute-start(bf16[512,256]{1,0:T(8,128)(2,1)S(1)} %collective-permute-done.10.refs_17_), channel_id=1, source_target_pairs={{0,32},{8,488},{32,64},{40,8},{64,96},{72,40},{96,128},{104,72},{1... | collective-permute-start | bytes 786440 | tf_op jit(solution)/shard_map/ppermute | solution.py:35
  72.7 2.8 %collective-permute-start.13 = (bf16[512,256]{1,0:T(8,128)(2,1)S(1)}, bf16[512,256]{1,0:T(8,128)(2,1)}, u32[]{:S(2)}, u32[]{:S(2)}) collective-permute-start(bf16[512,256]{1,0:T(8,128)(2,1)S(1)} %collective-permute-done.11.refs_18_), channel_id=1, source_target_pairs={{0,32},{8,488},{32,64},{40,8},{64,96},{72,40},{96,128},{104,72},{1... | collective-permute-start | bytes 786440 | tf_op jit(solution)/shard_map/ppermute | solution.py:35
  76.2 6.2 %collective-permute-start.15 = (bf16[3072,256]{1,0:T(8,128)(2,1)}, bf16[3072,256]{1,0:T(8,128)(2,1)S(1)}, u32[]{:S(2)}, u32[]{:S(2)}) collective-permute-start(bf16[3072,256]{1,0:T(8,128)(2,1)} %constant_dynamic-update-slice_fusion), channel_id=1, source_target_pairs={{0,8},{8,0},{1,9},{9,1},{2,10},{10,2},{3,11},{11,3},{4,12},{12,4},... | collective-permute-start | bytes 4718600 | tf_op jit(solution)/shard_map/ppermute | solution.py:39
  86.6 4.7 %collective-permute-start.16 = (bf16[2048,256]{1,0:T(8,128)(2,1)}, bf16[2048,256]{1,0:T(8,128)(2,1)}, u32[]{:S(2)}, u32[]{:S(2)}) collective-permute-start(bf16[2048,256]{1,0:T(8,128)(2,1)} %pad_maximum_fusion.1), channel_id=1, source_target_pairs={{0,8},{8,0},{1,9},{9,1},{2,10},{10,2},{3,11},{11,3},{4,12},{12,4},... | collective-permute-start | bytes 3145736 | tf_op jit(solution)/shard_map/ppermute | solution.py:39
  91.9 2.8 %collective-permute-start.17 = (bf16[512,256]{1,0:T(8,128)(2,1)}, bf16[512,256]{1,0:T(8,128)(2,1)S(1)}, u32[]{:S(2)}, u32[]{:S(2)}) collective-permute-start(bf16[512,256]{1,0:T(8,128)(2,1)} %collective-permute-done.12.refs_19_), channel_id=1, source_target_pairs={{0,32},{8,488},{32,64},{40,8},{64,96},{72,40},{96,128},{104,72},{1... | collective-permute-start | bytes 786440 | tf_op jit(solution)/shard_map/ppermute | solution.py:35
  99.6 2.9 %collective-permute-done.18.refs_25_ = bf16[512,256]{1,0:T(8,128)(2,1)} collective-permute-done((bf16[512,256]{1,0:T(8,128)(2,1)}, bf16[512,256]{1,0:T(8,128)(2,1)}, u32[]{:S(2)}, u32[]{:S(2)}) %collective-permute-start.18) | collective-permute-done | bytes 262176 | tf_op jit(solution)/shard_map/ppermute | solution.py:35
  105.6 9.9 %forward.1 = (f32[2,128,512]{2,1,0:T(8,128)S(1)}, f32[2,2688,512]{2,1,0:T(8,128)S(1)}, bf16[5504,256]{1,0:T(8,128)(2,1)S(1)}, f32[8,4,128]{2,1,0:T(4,128)S(1)}) custom-call(s32[2,21]{1,0:T(2,128)S(1)} %compare_select_fusion.7.refs_0_, s32[128]{0:T(128)S(1)} %get-tuple-element.77.refs_1_, bf16[256,512]{1,0:T(8,128)(2,1)S(1)} %copy-done.3, ...), custom_call_target="tpu_custom_call" | custom-call | flops 1409286144 | bytes 16777216 | tf_op jit(solution)/shard_map/forward/pallas_call | solution.py:364
  115.5 9.6 %all_to_all.5.refs_2_.refs_1_ = f32[8,4,128]{2,1,0:T(4,128)S(1)} all-to-all(f32[8,4,128]{2,1,0:T(4,128)S(1)} %get-tuple-element.40), channel_id=1, replica_groups=mesh['z'=16,'xh'=2,'core'=2,'y'=4,'xl'=2] {'y','xl'}, dimensions={0} | all-to-all | bytes 32768 | tf_op jit(solution)/shard_map/all_to_all | solution.py:102
  125.0 9.0 %backward.1 = (bf16[2,2688,512]{2,1,0:T(8,128)(2,1)S(1)}, bf16[8192,256]{1,0:T(8,128)(2,1)S(1)}, bf16[3072,256]{1,0:T(8,128)(2,1)S(1)}, bf16[2048,256]{1,0:T(8,1...) custom-call(s32[2,21]{1,0:T(2,128)S(1)} %compare_select_fusion.7.refs_0_, ...), custom_call_target="tpu_custom_call" | custom-call | flops 2113929216 | bytes 33554432 | tf_op jit(solution)/shard_map/backward/pallas_call | solution.py:385
  136.5 4.9 %collective-permute-start.21 = (bf16[2048,256]{1,0:T(8,128)(2,1)S(1)}, bf16[2048,256]{1,0:T(8,128)(2,1)S(1)}, u32[]{:S(2)}, u32[]{:S(2)}) collective-permute-start(bf16[2048,256]{1,0:T(8,128)(2,1)S(1)} %get-tuple-element.50), channel_id=1, source_target_pairs={{0,8},{8,0},{1,9},{9,1},{2,10},{10,2},{3,11},{11,3},{4,12},{12,4},... | collective-permute-start | bytes 3145736 | tf_op jit(solution)/shard_map/ppermute | solution.py:39
  141.4 2.9 %collective-permute-start.20 = (bf16[512,256]{1,0:T(8,128)(2,1)S(1)}, bf16[512,256]{1,0:T(8,128)(2,1)S(1)}, u32[]{:S(2)}, u32[]{:S(2)}) collective-permute-start(bf16[512,256]{1,0:T(8,128)(2,1)S(1)} %get-tuple-element.48), channel_id=1, source_target_pairs={{0,32},{8,488},{32,64},{40,8},{64,96},{72,40},{96,128},{104,72},{1... | collective-permute-start | bytes 786440 | tf_op jit(solution)/shard_map/ppermute | solution.py:35
  146.2 3.9 %collective-permute-start.19 = (bf16[512,256]{1,0:T(8,128)(2,1)S(1)}, bf16[512,256]{1,0:T(8,128)(2,1)S(1)}, u32[]{:S(2)}, u32[]{:S(2)}) collective-permute-start(bf16[512,256]{1,0:T(8,128)(2,1)S(1)} %get-tuple-element.47), channel_id=1, source_target_pairs={{0,32},{8,488},{32,64},{40,8},{64,96},{72,40},{96,128},{104,72},{1... | collective-permute-start | bytes 786440 | tf_op jit(solution)/shard_map/ppermute | solution.py:35
  155.0 4.9 %collective-permute-start.22 = (bf16[512,256]{1,0:T(8,128)(2,1)S(1)}, bf16[512,256]{1,0:T(8,128)(2,1)S(1)}, u32[]{:S(2)}, u32[]{:S(2)}) collective-permute-start(bf16[512,256]{1,0:T(8,128)(2,1)S(1)} %add_convert_fusion.13), channel_id=1, source_target_pairs={{0,32},{8,488},{32,64},{40,8},{64,96},{72,40},{96,128},{104,72},{1... | collective-permute-start | bytes 786440 | tf_op jit(solution)/shard_map/ppermute | solution.py:35
  163.2 5.0 %collective-permute-start.24 = (bf16[512,256]{1,0:T(8,128)(2,1)S(1)}, bf16[512,256]{1,0:T(8,128)(2,1)S(1)}, u32[]{:S(2)}, u32[]{:S(2)}) collective-permute-start(bf16[512,256]{1,0:T(8,128)(2,1)S(1)} %add_convert_fusion.11), channel_id=1, source_target_pairs={{0,32},{8,488},{32,64},{40,8},{64,96},{72,40},{96,128},{104,72},{1... | collective-permute-start | bytes 786440 | tf_op jit(solution)/shard_map/ppermute | solution.py:35
  171.7 5.0 %collective-permute-start.27 = (bf16[512,256]{1,0:T(8,128)(2,1)S(1)}, bf16[512,256]{1,0:T(8,128)(2,1)S(1)}, u32[]{:S(2)}, u32[]{:S(2)}) collective-permute-start(bf16[512,256]{1,0:T(8,128)(2,1)S(1)} %add_convert_fusion.9), channel_id=1, source_target_pairs={{0,32},{8,488},{32,64},{40,8},{64,96},{72,40},{96,128},{104,72},{1... | collective-permute-start | bytes 786440 | tf_op jit(solution)/shard_map/ppermute | solution.py:35
  180.1 5.0 %collective-permute-start.29 = (bf16[512,256]{1,0:T(8,128)(2,1)S(1)}, bf16[512,256]{1,0:T(8,128)(2,1)S(1)}, u32[]{:S(2)}, u32[]{:S(2)}) collective-permute-start(bf16[512,256]{1,0:T(8,128)(2,1)S(1)} %add_convert_fusion.7), channel_id=1, source_target_pairs={{0,32},{8,488},{32,64},{40,8},{64,96},{72,40},{96,128},{104,72},{1... | collective-permute-start | bytes 786440 | tf_op jit(solution)/shard_map/ppermute | solution.py:35
  188.5 5.0 %collective-permute-start.32 = (bf16[512,256]{1,0:T(8,128)(2,1)S(1)}, bf16[512,256]{1,0:T(8,128)(2,1)S(1)}, u32[]{:S(2)}, u32[]{:S(2)}) collective-permute-start(bf16[512,256]{1,0:T(8,128)(2,1)S(1)} %add_convert_fusion.5), channel_id=1, source_target_pairs={{0,32},{8,488},{32,64},{40,8},{64,96},{72,40},{96,128},{104,72},{1... | collective-permute-start | bytes 786440 | tf_op jit(solution)/shard_map/ppermute | solution.py:35
  197.0 5.0 %collective-permute-start.34 = (bf16[512,256]{1,0:T(8,128)(2,1)S(1)}, bf16[512,256]{1,0:T(8,128)(2,1)S(1)}, u32[]{:S(2)}, u32[]{:S(2)}) collective-permute-start(bf16[512,256]{1,0:T(8,128)(2,1)S(1)} %add_convert_fusion.3), channel_id=1, source_target_pairs={{0,32},{8,488},{32,64},{40,8},{64,96},{72,40},{96,128},{104,72},{1... | collective-permute-start | bytes 786440 | tf_op jit(solution)/shard_map/ppermute | solution.py:35
  206.1 5.0 %collective-permute-start.36 = (bf16[512,256]{1,0:T(8,128)(2,1)}, bf16[512,256]{1,0:T(8,128)(2,1)}, u32[]{:S(2)}, u32[]{:S(2)}) collective-permute-start(bf16[512,256]{1,0:T(8,128)(2,1)} %add_convert_fusion.1), channel_id=1, source_target_pairs={{0,32},{8,488},{32,64},{40,8},{64,96},{72,40},{96,128},{104,72},{1... | collective-permute-start | bytes 786440 | tf_op jit(solution)/shard_map/ppermute | solution.py:35
  211.9 8.7 %collective-permute-start.38 = (bf16[512,256]{1,0:T(8,128)(2,1)}, bf16[512,256]{1,0:T(8,128)(2,1)}, u32[]{:S(2)}, u32[]{:S(2)}) collective-permute-start(bf16[512,256]{1,0:T(8,128)(2,1)} %add_convert_fusion), channel_id=1, source_target_pairs={{0,8},{8,0},{1,9},{9,1},{2,10},{10,2},{3,11},{11,3},{4,12},{12,4},... | collective-permute-start | bytes 786440 | tf_op jit(solution)/shard_map/ppermute | solution.py:39
  226.8 7.2 %all-gather.1 = bf16[512,256]{1,0:T(8,128)(2,1)S(1)} all-gather(bf16[256,256]{1,0:T(8,128)(2,1)S(1)} %select_convert_fusion), channel_id=3, replica_groups=mesh['z'=16,'xh'=2,'core'=2,'y'=4,'xl'=2] {'xh'}, dimensions={0}, use_global_device_ids=true | all-gather | bytes 393216 | tf_op jit(solution)/shard_map/all_gather | solution.py:97
  (150 shorter events, 65.3 us)
Async XLA Ops:
  16.3 9.8 %collective-permute-start = (bf16[512,256]{1,0:T(8,128)(2,1)S(1)}, bf16[512,256]{1,0:T(8,128)(2,1)S(1)}, u32[]{:S(2)}, u32[]{:S(2)}) collective-permute-start(bf16[512,256]{1,0:T(8,128)(2,1)S(1)} %bitcast.14), channel_id=1, source_target_pairs={{0,32},{8,488},{32,64},{40,8},{64,96},{72,40},{96,128},{104,72},{1... | collective-permute-start | bytes 786440 | tf_op jit(solution)/shard_map/ppermute | solution.py:35
  22.8 8.3 %collective-permute-start.1 = (bf16[512,256]{1,0:T(8,128)(2,1)S(1)}, bf16[512,256]{1,0:T(8,128)(2,1)S(1)}, u32[]{:S(2)}, u32[]{:S(2)}) collective-permute-start(bf16[512,256]{1,0:T(8,128)(2,1)S(1)} %bitcast.12), channel_id=1, source_target_pairs={{0,32},{8,488},{32,64},{40,8},{64,96},{72,40},{96,128},{104,72},{1... | collective-permute-start | bytes 786440 | tf_op jit(solution)/shard_map/ppermute | solution.py:35
  26.1 8.3 %collective-permute-start.2 = (bf16[512,256]{1,0:T(8,128)(2,1)S(1)}, bf16[512,256]{1,0:T(8,128)(2,1)S(1)}, u32[]{:S(2)}, u32[]{:S(2)}) collective-permute-start(bf16[512,256]{1,0:T(8,128)(2,1)S(1)} %collective-permute-done.refs_7_), channel_id=1, source_target_pairs={{0,32},{8,488},{32,64},{40,8},{64,96},{72,40},{96,128},{104,72},{1... | collective-permute-start | bytes 786440 | tf_op jit(solution)/shard_map/ppermute | solution.py:35
  34.4 8.7 %collective-permute-start.4 = (bf16[512,256]{1,0:T(8,128)(2,1)S(1)}, bf16[512,256]{1,0:T(8,128)(2,1)S(1)}, u32[]{:S(2)}, u32[]{:S(2)}) collective-permute-start(bf16[512,256]{1,0:T(8,128)(2,1)S(1)} %collective-permute-done.2.refs_9_), channel_id=1, source_target_pairs={{0,32},{8,488},{32,64},{40,8},{64,96},{72,40},{96,128},{104,72},{1... | collective-permute-start | bytes 786440 | tf_op jit(solution)/shard_map/ppermute | solution.py:35
  39.4 8.3 %collective-permute-start.5 = (bf16[512,256]{1,0:T(8,128)(2,1)S(1)}, bf16[512,256]{1,0:T(8,128)(2,1)S(1)}, u32[]{:S(2)}, u32[]{:S(2)}) collective-permute-start(bf16[512,256]{1,0:T(8,128)(2,1)S(1)} %collective-permute-done.3.refs_10_), channel_id=1, source_target_pairs={{0,32},{8,488},{32,64},{40,8},{64,96},{72,40},{96,128},{104,72},{1... | collective-permute-start | bytes 786440 | tf_op jit(solution)/shard_map/ppermute | solution.py:35
  43.0 8.7 %collective-permute-start.6 = (bf16[512,256]{1,0:T(8,128)(2,1)S(1)}, bf16[512,256]{1,0:T(8,128)(2,1)S(1)}, u32[]{:S(2)}, u32[]{:S(2)}) collective-permute-start(bf16[512,256]{1,0:T(8,128)(2,1)S(1)} %collective-permute-done.4.refs_11_), channel_id=1, source_target_pairs={{0,32},{8,488},{32,64},{40,8},{64,96},{72,40},{96,128},{104,72},{1... | collective-permute-start | bytes 786440 | tf_op jit(solution)/shard_map/ppermute | solution.py:35
  51.8 9.6 %collective-permute-start.8 = (bf16[512,256]{1,0:T(8,128)(2,1)S(1)}, bf16[512,256]{1,0:T(8,128)(2,1)S(1)}, u32[]{:S(2)}, u32[]{:S(2)}) collective-permute-start(bf16[512,256]{1,0:T(8,128)(2,1)S(1)} %collective-permute-done.6.refs_13_), channel_id=1, source_target_pairs={{0,32},{8,488},{32,64},{40,8},{64,96},{72,40},{96,128},{104,72},{1... | collective-permute-start | bytes 786440 | tf_op jit(solution)/shard_map/ppermute | solution.py:35
  64.4 8.3 %collective-permute-start.11 = (bf16[512,256]{1,0:T(8,128)(2,1)S(1)}, bf16[512,256]{1,0:T(8,128)(2,1)S(1)}, u32[]{:S(2)}, u32[]{:S(2)}) collective-permute-start(bf16[512,256]{1,0:T(8,128)(2,1)S(1)} %collective-permute-done.9.refs_16_), channel_id=1, source_target_pairs={{0,32},{8,488},{32,64},{40,8},{64,96},{72,40},{96,128},{104,72},{1... | collective-permute-start | bytes 786440 | tf_op jit(solution)/shard_map/ppermute | solution.py:35
  69.3 15.1 %collective-permute-start.12 = (bf16[512,256]{1,0:T(8,128)(2,1)S(1)}, bf16[512,256]{1,0:T(8,128)(2,1)}, u32[]{:S(2)}, u32[]{:S(2)}) collective-permute-start(bf16[512,256]{1,0:T(8,128)(2,1)S(1)} %collective-permute-done.10.refs_17_), channel_id=1, source_target_pairs={{0,32},{8,488},{32,64},{40,8},{64,96},{72,40},{96,128},{104,72},{1... | collective-permute-start | bytes 786440 | tf_op jit(solution)/shard_map/ppermute | solution.py:35
  72.7 11.8 %collective-permute-start.13 = (bf16[512,256]{1,0:T(8,128)(2,1)S(1)}, bf16[512,256]{1,0:T(8,128)(2,1)}, u32[]{:S(2)}, u32[]{:S(2)}) collective-permute-start(bf16[512,256]{1,0:T(8,128)(2,1)S(1)} %collective-permute-done.11.refs_18_), channel_id=1, source_target_pairs={{0,32},{8,488},{32,64},{40,8},{64,96},{72,40},{96,128},{104,72},{1... | collective-permute-start | bytes 786440 | tf_op jit(solution)/shard_map/ppermute | solution.py:35
  76.2 26.2 %collective-permute-start.15 = (bf16[3072,256]{1,0:T(8,128)(2,1)}, bf16[3072,256]{1,0:T(8,128)(2,1)S(1)}, u32[]{:S(2)}, u32[]{:S(2)}) collective-permute-start(bf16[3072,256]{1,0:T(8,128)(2,1)} %constant_dynamic-update-slice_fusion), channel_id=1, source_target_pairs={{0,8},{8,0},{1,9},{9,1},{2,10},{10,2},{3,11},{11,3},{4,12},{12,4},... | collective-permute-start | bytes 4718600 | tf_op jit(solution)/shard_map/ppermute | solution.py:39
  82.5 15.0 %collective-permute-start.14 = (bf16[2048,256]{1,0:T(8,128)(2,1)S(1)}, bf16[2048,256]{1,0:T(8,128)(2,1)}, u32[]{:S(2)}, u32[]{:S(2)}) collective-permute-start(bf16[2048,256]{1,0:T(8,128)(2,1)S(1)} %pad_maximum_fusion), channel_id=1, source_target_pairs={{0,8},{8,0},{1,9},{9,1},{2,10},{10,2},{3,11},{11,3},{4,12},{12,4},... | collective-permute-start | bytes 3145736 | tf_op jit(solution)/shard_map/ppermute | solution.py:39
  86.6 15.9 %collective-permute-start.16 = (bf16[2048,256]{1,0:T(8,128)(2,1)}, bf16[2048,256]{1,0:T(8,128)(2,1)}, u32[]{:S(2)}, u32[]{:S(2)}) collective-permute-start(bf16[2048,256]{1,0:T(8,128)(2,1)} %pad_maximum_fusion.1), channel_id=1, source_target_pairs={{0,8},{8,0},{1,9},{9,1},{2,10},{10,2},{3,11},{11,3},{4,12},{12,4},... | collective-permute-start | bytes 3145736 | tf_op jit(solution)/shard_map/ppermute | solution.py:39
  136.5 13.7 %collective-permute-start.21 = (bf16[2048,256]{1,0:T(8,128)(2,1)S(1)}, bf16[2048,256]{1,0:T(8,128)(2,1)S(1)}, u32[]{:S(2)}, u32[]{:S(2)}) collective-permute-start(bf16[2048,256]{1,0:T(8,128)(2,1)S(1)} %get-tuple-element.50), channel_id=1, source_target_pairs={{0,8},{8,0},{1,9},{9,1},{2,10},{10,2},{3,11},{11,3},{4,12},{12,4},... | collective-permute-start | bytes 3145736 | tf_op jit(solution)/shard_map/ppermute | solution.py:39
  141.4 8.7 %collective-permute-start.20 = (bf16[512,256]{1,0:T(8,128)(2,1)S(1)}, bf16[512,256]{1,0:T(8,128)(2,1)S(1)}, u32[]{:S(2)}, u32[]{:S(2)}) collective-permute-start(bf16[512,256]{1,0:T(8,128)(2,1)S(1)} %get-tuple-element.48), channel_id=1, source_target_pairs={{0,32},{8,488},{32,64},{40,8},{64,96},{72,40},{96,128},{104,72},{1... | collective-permute-start | bytes 786440 | tf_op jit(solution)/shard_map/ppermute | solution.py:35
  144.3 24.0 %collective-permute-start.26 = (bf16[2048,256]{1,0:T(8,128)(2,1)S(1)}, bf16[2048,256]{1,0:T(8,128)(2,1)S(1)}, u32[]{:S(2)}, u32[]{:S(2)}) collective-permute-start(bf16[2048,256]{1,0:T(8,128)(2,1)S(1)} %get-tuple-element.57), channel_id=1, source_target_pairs={{0,8},{8,0},{1,9},{9,1},{2,10},{10,2},{3,11},{11,3},{4,12},{12,4},... | collective-permute-start | bytes 3145736 | tf_op jit(solution)/shard_map/ppermute | solution.py:39
  146.2 8.7 %collective-permute-start.19 = (bf16[512,256]{1,0:T(8,128)(2,1)S(1)}, bf16[512,256]{1,0:T(8,128)(2,1)S(1)}, u32[]{:S(2)}, u32[]{:S(2)}) collective-permute-start(bf16[512,256]{1,0:T(8,128)(2,1)S(1)} %get-tuple-element.47), channel_id=1, source_target_pairs={{0,32},{8,488},{32,64},{40,8},{64,96},{72,40},{96,128},{104,72},{1... | collective-permute-start | bytes 786440 | tf_op jit(solution)/shard_map/ppermute | solution.py:35
  150.3 9.6 %collective-permute-start.23 = (bf16[512,256]{1,0:T(8,128)(2,1)S(1)}, bf16[512,256]{1,0:T(8,128)(2,1)S(1)}, u32[]{:S(2)}, u32[]{:S(2)}) collective-permute-start(bf16[512,256]{1,0:T(8,128)(2,1)S(1)} %add_convert_fusion.14), channel_id=1, source_target_pairs={{0,32},{8,488},{32,64},{40,8},{64,96},{72,40},{96,128},{104,72},{1... | collective-permute-start | bytes 786440 | tf_op jit(solution)/shard_map/ppermute | solution.py:35
  152.7 32.4 %collective-permute-start.31 = (bf16[3072,256]{1,0:T(8,128)(2,1)S(1)}, bf16[3072,256]{1,0:T(8,128)(2,1)S(1)}, u32[]{:S(2)}, u32[]{:S(2)}) collective-permute-start(bf16[3072,256]{1,0:T(8,128)(2,1)S(1)} %get-tuple-element.64), channel_id=1, source_target_pairs={{0,8},{8,0},{1,9},{9,1},{2,10},{10,2},{3,11},{11,3},{4,12},{12,4},... | collective-permute-start | bytes 4718600 | tf_op jit(solution)/shard_map/ppermute | solution.py:39
  160.0 8.3 %collective-permute-start.25 = (bf16[512,256]{1,0:T(8,128)(2,1)S(1)}, bf16[512,256]{1,0:T(8,128)(2,1)S(1)}, u32[]{:S(2)}, u32[]{:S(2)}) collective-permute-start(bf16[512,256]{1,0:T(8,128)(2,1)S(1)} %add_convert_fusion.12), channel_id=1, source_target_pairs={{0,32},{8,488},{32,64},{40,8},{64,96},{72,40},{96,128},{104,72},{1... | collective-permute-start | bytes 786440 | tf_op jit(solution)/shard_map/ppermute | solution.py:35
  163.2 8.3 %collective-permute-start.24 = (bf16[512,256]{1,0:T(8,128)(2,1)S(1)}, bf16[512,256]{1,0:T(8,128)(2,1)S(1)}, u32[]{:S(2)}, u32[]{:S(2)}) collective-permute-start(bf16[512,256]{1,0:T(8,128)(2,1)S(1)} %add_convert_fusion.11), channel_id=1, source_target_pairs={{0,32},{8,488},{32,64},{40,8},{64,96},{72,40},{96,128},{104,72},{1... | collective-permute-start | bytes 786440 | tf_op jit(solution)/shard_map/ppermute | solution.py:35
  168.4 8.3 %collective-permute-start.28 = (bf16[512,256]{1,0:T(8,128)(2,1)S(1)}, bf16[512,256]{1,0:T(8,128)(2,1)S(1)}, u32[]{:S(2)}, u32[]{:S(2)}) collective-permute-start(bf16[512,256]{1,0:T(8,128)(2,1)S(1)} %add_convert_fusion.10), channel_id=1, source_target_pairs={{0,32},{8,488},{32,64},{40,8},{64,96},{72,40},{96,128},{104,72},{1... | collective-permute-start | bytes 786440 | tf_op jit(solution)/shard_map/ppermute | solution.py:35
  171.7 8.3 %collective-permute-start.27 = (bf16[512,256]{1,0:T(8,128)(2,1)S(1)}, bf16[512,256]{1,0:T(8,128)(2,1)S(1)}, u32[]{:S(2)}, u32[]{:S(2)}) collective-permute-start(bf16[512,256]{1,0:T(8,128)(2,1)S(1)} %add_convert_fusion.9), channel_id=1, source_target_pairs={{0,32},{8,488},{32,64},{40,8},{64,96},{72,40},{96,128},{104,72},{1... | collective-permute-start | bytes 786440 | tf_op jit(solution)/shard_map/ppermute | solution.py:35
  176.8 8.3 %collective-permute-start.30 = (bf16[512,256]{1,0:T(8,128)(2,1)S(1)}, bf16[512,256]{1,0:T(8,128)(2,1)S(1)}, u32[]{:S(2)}, u32[]{:S(2)}) collective-permute-start(bf16[512,256]{1,0:T(8,128)(2,1)S(1)} %add_convert_fusion.8), channel_id=1, source_target_pairs={{0,32},{8,488},{32,64},{40,8},{64,96},{72,40},{96,128},{104,72},{1... | collective-permute-start | bytes 786440 | tf_op jit(solution)/shard_map/ppermute | solution.py:35
  180.1 8.3 %collective-permute-start.29 = (bf16[512,256]{1,0:T(8,128)(2,1)S(1)}, bf16[512,256]{1,0:T(8,128)(2,1)S(1)}, u32[]{:S(2)}, u32[]{:S(2)}) collective-permute-start(bf16[512,256]{1,0:T(8,128)(2,1)S(1)} %add_convert_fusion.7), channel_id=1, source_target_pairs={{0,32},{8,488},{32,64},{40,8},{64,96},{72,40},{96,128},{104,72},{1... | collective-permute-start | bytes 786440 | tf_op jit(solution)/shard_map/ppermute | solution.py:35
  185.3 8.3 %collective-permute-start.33 = (bf16[512,256]{1,0:T(8,128)(2,1)S(1)}, bf16[512,256]{1,0:T(8,128)(2,1)S(1)}, u32[]{:S(2)}, u32[]{:S(2)}) collective-permute-start(bf16[512,256]{1,0:T(8,128)(2,1)S(1)} %add_convert_fusion.6), channel_id=1, source_target_pairs={{0,32},{8,488},{32,64},{40,8},{64,96},{72,40},{96,128},{104,72},{1... | collective-permute-start | bytes 786440 | tf_op jit(solution)/shard_map/ppermute | solution.py:35
  188.5 8.3 %collective-permute-start.32 = (bf16[512,256]{1,0:T(8,128)(2,1)S(1)}, bf16[512,256]{1,0:T(8,128)(2,1)S(1)}, u32[]{:S(2)}, u32[]{:S(2)}) collective-permute-start(bf16[512,256]{1,0:T(8,128)(2,1)S(1)} %add_convert_fusion.5), channel_id=1, source_target_pairs={{0,32},{8,488},{32,64},{40,8},{64,96},{72,40},{96,128},{104,72},{1... | collective-permute-start | bytes 786440 | tf_op jit(solution)/shard_map/ppermute | solution.py:35
  193.7 8.3 %collective-permute-start.35 = (bf16[512,256]{1,0:T(8,128)(2,1)S(1)}, bf16[512,256]{1,0:T(8,128)(2,1)S(1)}, u32[]{:S(2)}, u32[]{:S(2)}) collective-permute-start(bf16[512,256]{1,0:T(8,128)(2,1)S(1)} %add_convert_fusion.4), channel_id=1, source_target_pairs={{0,32},{8,488},{32,64},{40,8},{64,96},{72,40},{96,128},{104,72},{1... | collective-permute-start | bytes 786440 | tf_op jit(solution)/shard_map/ppermute | solution.py:35
  197.0 8.3 %collective-permute-start.34 = (bf16[512,256]{1,0:T(8,128)(2,1)S(1)}, bf16[512,256]{1,0:T(8,128)(2,1)S(1)}, u32[]{:S(2)}, u32[]{:S(2)}) collective-permute-start(bf16[512,256]{1,0:T(8,128)(2,1)S(1)} %add_convert_fusion.3), channel_id=1, source_target_pairs={{0,32},{8,488},{32,64},{40,8},{64,96},{72,40},{96,128},{104,72},{1... | collective-permute-start | bytes 786440 | tf_op jit(solution)/shard_map/ppermute | solution.py:35
  202.1 9.0 %collective-permute-start.37 = (bf16[512,256]{1,0:T(8,128)(2,1)S(1)}, bf16[512,256]{1,0:T(8,128)(2,1)S(1)}, u32[]{:S(2)}, u32[]{:S(2)}) collective-permute-start(bf16[512,256]{1,0:T(8,128)(2,1)S(1)} %add_convert_fusion.2), channel_id=1, source_target_pairs={{0,32},{8,488},{32,64},{40,8},{64,96},{72,40},{96,128},{104,72},{1... | collective-permute-start | bytes 786440 | tf_op jit(solution)/shard_map/ppermute | solution.py:35
  206.1 19.4 %collective-permute-start.36 = (bf16[512,256]{1,0:T(8,128)(2,1)}, bf16[512,256]{1,0:T(8,128)(2,1)}, u32[]{:S(2)}, u32[]{:S(2)}) collective-permute-start(bf16[512,256]{1,0:T(8,128)(2,1)} %add_convert_fusion.1), channel_id=1, source_target_pairs={{0,32},{8,488},{32,64},{40,8},{64,96},{72,40},{96,128},{104,72},{1... | collective-permute-start | bytes 786440 | tf_op jit(solution)/shard_map/ppermute | solution.py:35
  211.9 13.6 %collective-permute-start.38 = (bf16[512,256]{1,0:T(8,128)(2,1)}, bf16[512,256]{1,0:T(8,128)(2,1)}, u32[]{:S(2)}, u32[]{:S(2)}) collective-permute-start(bf16[512,256]{1,0:T(8,128)(2,1)} %add_convert_fusion), channel_id=1, source_target_pairs={{0,8},{8,0},{1,9},{9,1},{2,10},{10,2},{3,11},{11,3},{4,12},{12,4},... | collective-permute-start | bytes 786440 | tf_op jit(solution)/shard_map/ppermute | solution.py:39
  (33 other events, 577.1 us)
